TPU v7x, 256 devices: a whole 4x4x8 slice. The times are simulated.
256 devices in a mesh: gx: 4 (over x), gy: 4 (over y), gz: 16 (over z, core).
Axes of the slice: x: 4, y: 4, z: 8, core: 2. Of those that a mesh axis runs over, the one named last changes fastest.
Arguments:
- phase: int32 [32, 256, 2048], P('gx', 'gy', 'gz'), may hold values 0 or 1
- density: float32 [32, 256, 2048], P('gx', 'gy', 'gz'), may hold values from 0.5 to 2
- rhs: float32 [1, 32, 256, 2048], P(None, 'gx', 'gy', 'gz'), may hold values from -6 to 6
Outputs:
- scaled_solution: float32 [1, 32, 256, 2048], P(None, 'gx', 'gy', 'gz')
- residual: float32 [1, 32, 256, 2048], P(None, 'gx', 'gy', 'gz')
All inputs are finite; a program needn't handle non-finite values. No bound on the sum of `phase` on one device may be relied on, other than what follows from the above.
Results may differ from a plain program's by a relative error of at most 0.0003.
Values sent between devices are 32-bit elements; how exact they have to be, the bound alone decides.
A program may use at most 128 MiB of HBM per device.

v0:
```python
import jax
import jax.numpy as jnp
from jax import lax
from jax.sharding import PartitionSpec as P

LEVELS = 4
SWEEPS = 2
COARSE_SWEEPS = 4


damping = 2.0 / 3.0


def padded_2(cells, sides, width):
    for axis, dim in sides:
        count = lax.axis_size(axis)
        ends = count - 1
        head = lax.slice_in_dim(cells, 0, width, axis=dim)
        tail = lax.slice_in_dim(cells, cells.shape[dim] - width, cells.shape[dim], axis=dim)
        cells = jnp.concatenate(
            [
                lax.ppermute(tail, axis, [(i, (i + 1) % count) for i in range(ends)]),
                cells,
                lax.ppermute(head, axis, [((i + 1) % count, i) for i in range(ends)]),
            ],
            axis=dim,
        )
    return cells


def face_pair(rho, up_nb, down_nb, top, bottom):
    face_up = 2.0 / (rho + up_nb)
    face_down = 2.0 / (rho + down_nb)
    return (face_up, face_down, jnp.where(top, 0.0, face_up), jnp.where(bottom, 0.0, face_down))


def side_masks(where_now, axis_count, count, shape, dim):
    row = lax.broadcasted_iota(jnp.int32, shape, dim)
    top = (row == count - 1) & (where_now == axis_count - 1)
    bottom = (row == 0) & (where_now == 0)
    return (top, bottom)


def make_coef(rho):
    nx, ny, nz = rho.shape
    ext = padded_2(rho, (("gx", 0), ("gy", 1), ("gz", 2)), 1)
    top_x, bot_x = side_masks(lax.axis_index("gx"), lax.axis_size("gx"), nx, (nx, 1, 1), 0)
    top_y, bot_y = side_masks(lax.axis_index("gy"), lax.axis_size("gy"), ny, (1, ny, 1), 1)
    top_z, bot_z = side_masks(lax.axis_index("gz"), lax.axis_size("gz"), nz, (1, 1, nz), 2)
    fxu, fxd, kxu, kxd = face_pair(
        rho,
        jnp.where(top_x, rho, ext[2:, 1:-1, 1:-1]),
        jnp.where(bot_x, rho, ext[:-2, 1:-1, 1:-1]),
        top_x,
        bot_x,
    )
    fyu, fyd, kyu, kyd = face_pair(
        rho,
        jnp.where(top_y, rho, ext[1:-1, 2:, 1:-1]),
        jnp.where(bot_y, rho, ext[1:-1, :-2, 1:-1]),
        top_y,
        bot_y,
    )
    fzu, fzd, kzu, kzd = face_pair(
        rho,
        jnp.where(top_z, rho, ext[1:-1, 1:-1, 2:]),
        jnp.where(bot_z, rho, ext[1:-1, 1:-1, :-2]),
        top_z,
        bot_z,
    )
    diag = fxu + fxd + fyu + fyd + fzu + fzd
    return jnp.stack([diag, kxu, kxd, kyu, kyd, kzu, kzd])


def blocks(a):
    s = a.shape
    lead = s[:-3]
    return a.reshape(lead + (s[-3] // 2, 2, s[-2] // 2, 2, s[-1] // 2, 2)).sum(axis=(-5, -3, -1))


def prolong(e):
    s = e.shape
    lead = s[:-3]
    wide = e.reshape(lead + (s[-3], 1, s[-2], 1, s[-1], 1))
    wide = jnp.broadcast_to(wide, lead + (s[-3], 2, s[-2], 2, s[-1], 2))
    return wide.reshape(lead + (2 * s[-3], 2 * s[-2], 2 * s[-1]))


def face_x(a, offset):
    b = a[offset::2]
    n0, n1, n2 = b.shape
    return b.reshape(n0, n1 // 2, 2, n2 // 2, 2).sum(axis=(2, 4))


def face_y(a, offset):
    b = a[:, offset::2]
    n0, n1, n2 = b.shape
    return b.reshape(n0 // 2, 2, n1, n2 // 2, 2).sum(axis=(1, 4))


def face_z(a, offset):
    b = a[:, :, offset::2]
    n0, n1, n2 = b.shape
    return b.reshape(n0 // 2, 2, n1 // 2, 2, n2).sum(axis=(1, 3))


def coarsen(coef):
    inner = face_x(coef[1], 0) + face_y(coef[3], 0) + face_z(coef[5], 0)
    diag = blocks(coef[0]) - 2.0 * inner
    return jnp.stack(
        [
            diag,
            face_x(coef[1], 1),
            face_x(coef[2], 0),
            face_y(coef[3], 1),
            face_y(coef[4], 0),
            face_z(coef[5], 1),
            face_z(coef[6], 0),
        ]
    )


def stencil(padded, field, coef):
    beside = coef[1] * padded[:, 2:, 1:-1, 1:-1] + coef[2] * padded[:, :-2, 1:-1, 1:-1]
    beside = beside + coef[3] * padded[:, 1:-1, 2:, 1:-1] + coef[4] * padded[:, 1:-1, :-2, 1:-1]
    beside = beside + coef[5] * padded[:, 1:-1, 1:-1, 2:] + coef[6] * padded[:, 1:-1, 1:-1, :-2]
    return coef[0] * field - beside


def pad_spread(field):
    return padded_2(field, (("gx", 1), ("gy", 2), ("gz", 3)), 1)


def sweep(field, source, coef, pad_fn, first):
    if first:
        change = source
    else:
        change = source - stencil(pad_fn(field), field, coef)
    return field + damping * change / coef[0]


def smooth_many(source, coef, pad_fn, count):
    field = jnp.zeros_like(source)
    for step in range(count):
        field = sweep(field, source, coef, pad_fn, step == 0)
    return field


def coarsest(source, coef):
    return smooth_many(source, coef, pad_spread, COARSE_SWEEPS)


def vcycle(level, source, coefs):
    coef = coefs[level]
    if level == LEVELS - 1:
        return coarsest(source, coef)
    field = smooth_many(source, coef, pad_spread, SWEEPS)
    remain = source - stencil(pad_spread(field), field, coef)
    correction = vcycle(level + 1, blocks(remain), coefs)
    field = field + prolong(correction)
    for step in range(SWEEPS):
        field = sweep(field, source, coef, pad_spread, False)
    return field


def on_device(phase, density, rhs):
    rho = jnp.where(phase == 1, 1000.0, 1.0).astype(jnp.float32) * density
    coefs = [make_coef(rho)]
    for level in range(LEVELS - 1):
        coefs.append(coarsen(coefs[-1]))
    solution = vcycle(0, rhs, coefs)
    scaled_solution = coefs[0][0] * solution
    residual = rhs - stencil(pad_spread(solution), solution, coefs[0])
    return (scaled_solution, residual)


def solution(mesh):
    in_specs = (P("gx", "gy", "gz"), P("gx", "gy", "gz"), P(None, "gx", "gy", "gz"))
    out_specs = (P(None, "gx", "gy", "gz"), P(None, "gx", "gy", "gz"))
    return jax.shard_map(
        on_device, mesh=mesh, in_specs=in_specs, out_specs=out_specs, check_vma=False
    )
```

profile of v0, /device:TPU:127, one launch (start us, length us, event | category | flops | bytes accessed | tf_op | source)
XLA Modules:
  0.0 621.9 jit_solution(7878298820433733540)
XLA Ops:
  15.2 5.1 collective-permute-start.4
  46.2 8.5 %collective-permute-start.11 = (f32[1,10,66,1]{3,2,1,0:T(8,128)S(1)}, f32[1,10,66,1]{3,2,1,0:T(8,128)S(1)}, u32[]{:S(2)}, u32[]{:S(2)}) collective-permute-start(f32[1,10,66,1]{3,2,1,0:T(8,128)S(1)} %get-tuple-element.30), channel_id=1, source_target_pairs={{0,1},{1,2},{2,3},{3,4},{4,5},{5,6},{6,7},{7,8},{8,9},{9,10},{10,1... | collective-permute-start | bytes 7928 | tf_op jit(solution)/shard_map/ppermute | solution.py:22
  59.1 5.6 collective-permute-done.10
  75.9 18.1 %reshape_squeeze_stack.2 = f32[4,2,32,2,64,2]{5,4,3,2,1,0:T(8,128)} reshape(f32[8,64,128]{2,1,0:T(8,128)S(1)} %get-tuple-element.18) | data formatting | bytes 524288 | tf_op jit(solution)/shard_map/reshape;squeeze;stack | solution.py:78
  93.9 7.6 %reduce_sum.361 = f32[4,32,64]{2,1,0:T(8,128)} reduce(f32[4,2,32,2,64,2]{5,4,3,2,1,0:T(8,128)} %reshape_squeeze_stack.2, f32[]{:T(128)} %constant.11.clone.1), dimensions={1,3,5}, to_apply=%region_1.2 | reduce | flops 57344 | bytes 294916 | tf_op jit(solution)/shard_map/reduce_sum | solution.py:78
  116.8 5.6 reduce_sum.362
  125.7 18.1 %reshape.474 = f32[4,2,32,2,64,2]{5,4,3,2,1,0:T(8,128)} reshape(f32[1,8,64,128]{3,2,1,0:T(8,128)S(1)} %fusion.54) | data formatting | bytes 524288 | tf_op jit(solution)/shard_map/reshape | solution.py:78
  143.8 7.0 %reduce_sum.359 = f32[4,32,64]{2,1,0:T(8,128)S(1)} reduce(f32[4,2,32,2,64,2]{5,4,3,2,1,0:T(8,128)} %reshape.474, f32[]{:T(128)} %constant.11.clone.1), dimensions={1,3,5}, to_apply=%region_0.1 | reduce | flops 57344 | bytes 294916 | tf_op jit(solution)/shard_map/reduce_sum | solution.py:78
  159.4 4.9 collective-permute-start.20
  179.9 5.9 collective-permute-start.23
  191.1 5.6 reduce_sum.366
  201.2 5.6 reduce_sum.365
  219.2 5.0 collective-permute-start.26
  249.2 4.9 collective-permute-start.29
  278.8 5.5 slice.831
  299.5 5.8 collective-permute-start.35
  330.3 5.4 collective-permute-start.41
  355.8 4.7 collective-permute-start.47
  379.0 4.8 collective-permute-start.53
  402.3 4.8 collective-permute-start.59
  425.9 4.8 collective-permute-start.65
  432.6 4.7 collective-permute-done.64
  449.5 4.7 collective-permute-start.71
  456.2 4.7 collective-permute-done.70
  480.4 4.9 collective-permute-start.77
  505.7 7.0 %collective-permute-start.83 = (f32[1,6,34,1]{3,0,2,1:T(1,128)S(1)}, f32[1,6,34,1]{3,0,2,1:T(1,128)S(1)}, u32[]{:S(2)}, u32[]{:S(2)}) collective-permute-start(f32[1,6,34,1]{3,0,2,1:T(1,128)S(1)} %get-tuple-element.62), channel_id=1, source_target_pairs={{0,1},{1,2},{2,3},{3,4},{4,5},{5,6},{6,7},{7,8},{8,9},{9,10},{10,1... | collective-permute-start | bytes 2456 | tf_op jit(solution)/shard_map/ppermute | solution.py:22
  514.9 6.5 %broadcast_in_dim.131 = f32[4,2,32,2,64,2]{5,4,3,2,1,0:T(8,128)} broadcast(f32[4,32,64]{2,1,0:T(8,128)S(1)} %fusion.133), dimensions={0,2,4} | broadcast | bytes 294912 | tf_op jit(solution)/shard_map/broadcast_in_dim | solution.py:85
  521.4 12.6 %broadcast_in_dim.132 = f32[1,8,64,128]{3,2,1,0:T(8,128)S(1)} reshape(f32[4,2,32,2,64,2]{5,4,3,2,1,0:T(8,128)} %broadcast_in_dim.131) | data formatting | bytes 524288 | tf_op jit(solution)/shard_map/broadcast_in_dim | solution.py:85
  546.9 8.4 %collective-permute-start.89 = (f32[1,10,66,1]{3,2,1,0:T(8,128)S(1)}, f32[1,10,66,1]{3,2,1,0:T(8,128)S(1)}, u32[]{:S(2)}, u32[]{:S(2)}) collective-permute-start(f32[1,10,66,1]{3,2,1,0:T(8,128)S(1)} %get-tuple-element.26), channel_id=1, source_target_pairs={{0,1},{1,2},{2,3},{3,4},{4,5},{5,6},{6,7},{7,8},{8,9},{9,10},{10,1... | collective-permute-start | bytes 7928 | tf_op jit(solution)/shard_map/ppermute | solution.py:22
  559.7 5.6 collective-permute-done.88
  587.4 5.6 collective-permute-done.94
  615.0 5.6 collective-permute-done.100
  (425 shorter events, 405.4 us)
Async XLA Ops:
  15.2 13.1 %collective-permute-start.4 = (f32[10,66,1]{2,1,0:T(8,128)S(1)}, f32[10,66,1]{2,1,0:T(8,128)S(1)}, u32[]{:S(2)}, u32[]{:S(2)}) collective-permute-start(f32[10,66,1]{2,1,0:T(8,128)S(1)} %get-tuple-element.32), channel_id=1, source_target_pairs={{1,0},{2,1},{3,2},{4,3},{5,4},{6,5},{7,6},{8,7},{9,8},{10,9},{11,1... | collective-permute-start | bytes 7928 | tf_op jit(solution)/shard_map/ppermute | solution.py:24
  20.3 9.1 %collective-permute-start.5 = (f32[10,66,1]{2,1,0:T(8,128)S(1)}, f32[10,66,1]{2,1,0:T(8,128)S(1)}, u32[]{:S(2)}, u32[]{:S(2)}) collective-permute-start(f32[10,66,1]{2,1,0:T(8,128)S(1)} %get-tuple-element.31), channel_id=1, source_target_pairs={{0,1},{1,2},{2,3},{3,4},{4,5},{5,6},{6,7},{7,8},{8,9},{9,10},{10,1... | collective-permute-start | bytes 7928 | tf_op jit(solution)/shard_map/ppermute | solution.py:22
  46.2 12.9 %collective-permute-start.11 = (f32[1,10,66,1]{3,2,1,0:T(8,128)S(1)}, f32[1,10,66,1]{3,2,1,0:T(8,128)S(1)}, u32[]{:S(2)}, u32[]{:S(2)}) collective-permute-start(f32[1,10,66,1]{3,2,1,0:T(8,128)S(1)} %get-tuple-element.30), channel_id=1, source_target_pairs={{0,1},{1,2},{2,3},{3,4},{4,5},{5,6},{6,7},{7,8},{8,9},{9,10},{10,1... | collective-permute-start | bytes 7928 | tf_op jit(solution)/shard_map/ppermute | solution.py:22
  54.7 10.0 %collective-permute-start.10 = (f32[1,10,66,1]{3,2,1,0:T(8,128)S(1)}, f32[1,10,66,1]{3,2,1,0:T(8,128)S(1)}, u32[]{:S(2)}, u32[]{:S(2)}) collective-permute-start(f32[1,10,66,1]{3,2,1,0:T(8,128)S(1)} %get-tuple-element.29), channel_id=1, source_target_pairs={{1,0},{2,1},{3,2},{4,3},{5,4},{6,5},{7,6},{8,7},{9,8},{10,9},{11,1... | collective-permute-start | bytes 7928 | tf_op jit(solution)/shard_map/ppermute | solution.py:24
  72.2 29.4 %collective-permute-start.14 = (f32[1,10,1,128]{3,2,1,0:T(1,128)S(1)}, f32[1,10,1,128]{3,2,1,0:T(1,128)S(1)}, u32[]{:S(2)}, u32[]{:S(2)}) collective-permute-start(f32[1,10,1,128]{3,2,1,0:T(1,128)S(1)} %get-tuple-element.40), channel_id=1, source_target_pairs={{16,0},{32,16},{48,32},{17,1},{33,17},{49,33},{18,2},{34,18},{50,3... | collective-permute-start | bytes 15368 | tf_op jit(solution)/shard_map/ppermute | solution.py:24
  74.6 27.0 %collective-permute-start.15 = (f32[1,10,1,128]{3,2,1,0:T(1,128)S(1)}, f32[1,10,1,128]{3,2,1,0:T(1,128)S(1)}, u32[]{:S(2)}, u32[]{:S(2)}) collective-permute-start(f32[1,10,1,128]{3,2,1,0:T(1,128)S(1)} %get-tuple-element.39), channel_id=1, source_target_pairs={{0,16},{16,32},{32,48},{1,17},{17,33},{33,49},{2,18},{18,34},{34,5... | collective-permute-start | bytes 15368 | tf_op jit(solution)/shard_map/ppermute | solution.py:22
  102.6 21.7 %collective-permute-start.17 = (f32[1,10,66,1]{3,2,1,0:T(8,128)}, f32[1,10,66,1]{3,2,1,0:T(8,128)}, u32[]{:S(2)}, u32[]{:S(2)}) collective-permute-start(f32[1,10,66,1]{3,2,1,0:T(8,128)} %get-tuple-element.28), channel_id=1, source_target_pairs={{0,1},{1,2},{2,3},{3,4},{4,5},{5,6},{6,7},{7,8},{8,9},{9,10},{10,1... | collective-permute-start | bytes 7928 | tf_op jit(solution)/shard_map/ppermute | solution.py:22
  106.1 18.2 %collective-permute-start.16 = (f32[1,10,66,1]{3,2,1,0:T(8,128)}, f32[1,10,66,1]{3,2,1,0:T(8,128)}, u32[]{:S(2)}, u32[]{:S(2)}) collective-permute-start(f32[1,10,66,1]{3,2,1,0:T(8,128)} %get-tuple-element.27), channel_id=1, source_target_pairs={{1,0},{2,1},{3,2},{4,3},{5,4},{6,5},{7,6},{8,7},{9,8},{10,9},{11,1... | collective-permute-start | bytes 7928 | tf_op jit(solution)/shard_map/ppermute | solution.py:24
  158.1 18.2 %collective-permute-start.21 = (f32[1,6,1,64]{3,2,1,0:T(1,128)S(1)}, f32[1,6,1,64]{3,2,1,0:T(1,128)S(1)}, u32[]{:S(2)}, u32[]{:S(2)}) collective-permute-start(f32[1,6,1,64]{3,2,1,0:T(1,128)S(1)} %get-tuple-element.82), channel_id=1, source_target_pairs={{0,16},{16,32},{32,48},{1,17},{17,33},{33,49},{2,18},{18,34},{34,5... | collective-permute-start | bytes 4616 | tf_op jit(solution)/shard_map/ppermute | solution.py:22
  159.4 16.9 %collective-permute-start.20 = (f32[1,6,1,64]{3,2,1,0:T(1,128)S(1)}, f32[1,6,1,64]{3,2,1,0:T(1,128)S(1)}, u32[]{:S(2)}, u32[]{:S(2)}) collective-permute-start(f32[1,6,1,64]{3,2,1,0:T(1,128)S(1)} %get-tuple-element.81), channel_id=1, source_target_pairs={{16,0},{32,16},{48,32},{17,1},{33,17},{49,33},{18,2},{34,18},{50,3... | collective-permute-start | bytes 4616 | tf_op jit(solution)/shard_map/ppermute | solution.py:24
  177.4 30.5 %collective-permute-start.22 = (f32[1,6,34,1]{3,0,2,1:T(1,128)}, f32[1,6,34,1]{3,0,2,1:T(1,128)}, u32[]{:S(2)}, u32[]{:S(2)}) collective-permute-start(f32[1,6,34,1]{3,0,2,1:T(1,128)} %get-tuple-element.73), channel_id=1, source_target_pairs={{1,0},{2,1},{3,2},{4,3},{5,4},{6,5},{7,6},{8,7},{9,8},{10,9},{11,1... | collective-permute-start | bytes 2456 | tf_op jit(solution)/shard_map/ppermute | solution.py:24
  179.9 27.9 %collective-permute-start.23 = (f32[1,6,34,1]{3,0,2,1:T(1,128)}, f32[1,6,34,1]{3,0,2,1:T(1,128)}, u32[]{:S(2)}, u32[]{:S(2)}) collective-permute-start(f32[1,6,34,1]{3,0,2,1:T(1,128)} %get-tuple-element.74), channel_id=1, source_target_pairs={{0,1},{1,2},{2,3},{3,4},{4,5},{5,6},{6,7},{7,8},{8,9},{9,10},{10,1... | collective-permute-start | bytes 2456 | tf_op jit(solution)/shard_map/ppermute | solution.py:22
  218.0 28.0 %collective-permute-start.27 = (f32[1,6,1,64]{3,2,1,0:T(1,128)}, f32[1,6,1,64]{3,2,1,0:T(1,128)}, u32[]{:S(2)}, u32[]{:S(2)}) collective-permute-start(f32[1,6,1,64]{3,2,1,0:T(1,128)} %get-tuple-element.80), channel_id=1, source_target_pairs={{0,16},{16,32},{32,48},{1,17},{17,33},{33,49},{2,18},{18,34},{34,5... | collective-permute-start | bytes 4616 | tf_op jit(solution)/shard_map/ppermute | solution.py:22
  219.2 26.7 %collective-permute-start.26 = (f32[1,6,1,64]{3,2,1,0:T(1,128)}, f32[1,6,1,64]{3,2,1,0:T(1,128)}, u32[]{:S(2)}, u32[]{:S(2)}) collective-permute-start(f32[1,6,1,64]{3,2,1,0:T(1,128)} %get-tuple-element.79), channel_id=1, source_target_pairs={{16,0},{32,16},{48,32},{17,1},{33,17},{49,33},{18,2},{34,18},{50,3... | collective-permute-start | bytes 4616 | tf_op jit(solution)/shard_map/ppermute | solution.py:24
  247.3 8.8 %collective-permute-start.28 = (f32[1,6,34,1]{3,0,2,1:T(1,128)S(1)}, f32[1,6,34,1]{3,0,2,1:T(1,128)S(1)}, u32[]{:S(2)}, u32[]{:S(2)}) collective-permute-start(f32[1,6,34,1]{3,0,2,1:T(1,128)S(1)} %get-tuple-element.69), channel_id=1, source_target_pairs={{1,0},{2,1},{3,2},{4,3},{5,4},{6,5},{7,6},{8,7},{9,8},{10,9},{11,1... | collective-permute-start | bytes 2456 | tf_op jit(solution)/shard_map/ppermute | solution.py:24
  249.2 6.8 %collective-permute-start.29 = (f32[1,6,34,1]{3,0,2,1:T(1,128)S(1)}, f32[1,6,34,1]{3,0,2,1:T(1,128)S(1)}, u32[]{:S(2)}, u32[]{:S(2)}) collective-permute-start(f32[1,6,34,1]{3,0,2,1:T(1,128)S(1)} %get-tuple-element.70), channel_id=1, source_target_pairs={{0,1},{1,2},{2,3},{3,4},{4,5},{5,6},{6,7},{7,8},{8,9},{9,10},{10,1... | collective-permute-start | bytes 2456 | tf_op jit(solution)/shard_map/ppermute | solution.py:22
  267.4 21.2 %collective-permute-start.30 = (f32[1,1,16,32]{3,2,1,0:T(8,128)}, f32[1,1,16,32]{3,2,1,0:T(8,128)}, u32[]{:S(2)}, u32[]{:S(2)}) collective-permute-start(f32[1,1,16,32]{3,2,1,0:T(8,128)} %get-tuple-element.122), channel_id=1, source_target_pairs={{64,0},{128,64},{192,128},{65,1},{129,65},{193,129},{66,2},{130,66... | collective-permute-start | bytes 6152 | tf_op jit(solution)/shard_map/ppermute | solution.py:24
  269.9 18.7 %collective-permute-start.31 = (f32[1,1,16,32]{3,2,1,0:T(8,128)}, f32[1,1,16,32]{3,2,1,0:T(8,128)}, u32[]{:S(2)}, u32[]{:S(2)}) collective-permute-start(f32[1,1,16,32]{3,2,1,0:T(8,128)} %get-tuple-element.121), channel_id=1, source_target_pairs={{0,64},{64,128},{128,192},{1,65},{65,129},{129,193},{2,66},{66,130... | collective-permute-start | bytes 6152 | tf_op jit(solution)/shard_map/ppermute | solution.py:22
  289.3 9.3 %collective-permute-start.32 = (f32[1,4,1,32]{3,2,1,0:T(1,128)S(1)}, f32[1,4,1,32]{3,2,1,0:T(1,128)S(1)}, u32[]{:S(2)}, u32[]{:S(2)}) collective-permute-start(f32[1,4,1,32]{3,2,1,0:T(1,128)S(1)} %get-tuple-element.106), channel_id=1, source_target_pairs={{16,0},{32,16},{48,32},{17,1},{33,17},{49,33},{18,2},{34,18},{50,3... | collective-permute-start | bytes 1544 | tf_op jit(solution)/shard_map/ppermute | solution.py:24
  299.5 10.1 %collective-permute-start.35 = (f32[1,4,18,1]{3,2,1,0:T(8,128)S(1)}, f32[1,4,18,1]{3,2,1,0:T(8,128)S(1)}, u32[]{:S(2)}, u32[]{:S(2)}) collective-permute-start(f32[1,4,18,1]{3,2,1,0:T(8,128)S(1)} %get-tuple-element.98), channel_id=1, source_target_pairs={{0,1},{1,2},{2,3},{3,4},{4,5},{5,6},{6,7},{7,8},{8,9},{9,10},{10,1... | collective-permute-start | bytes 872 | tf_op jit(solution)/shard_map/ppermute | solution.py:22
  330.3 7.8 %collective-permute-start.41 = (f32[1,4,18,1]{3,2,1,0:T(8,128)S(1)}, f32[1,4,18,1]{3,2,1,0:T(8,128)S(1)}, u32[]{:S(2)}, u32[]{:S(2)}) collective-permute-start(f32[1,4,18,1]{3,2,1,0:T(8,128)S(1)} %get-tuple-element.96), channel_id=1, source_target_pairs={{0,1},{1,2},{2,3},{3,4},{4,5},{5,6},{6,7},{7,8},{8,9},{9,10},{10,1... | collective-permute-start | bytes 872 | tf_op jit(solution)/shard_map/ppermute | solution.py:22
  355.8 6.8 %collective-permute-start.47 = (f32[1,3,10,1]{3,2,1,0:T(8,128)S(1)}, f32[1,3,10,1]{3,2,1,0:T(8,128)S(1)}, u32[]{:S(2)}, u32[]{:S(2)}) collective-permute-start(f32[1,3,10,1]{3,2,1,0:T(8,128)S(1)} %get-tuple-element.112), channel_id=1, source_target_pairs={{0,1},{1,2},{2,3},{3,4},{4,5},{5,6},{6,7},{7,8},{8,9},{9,10},{10,1... | collective-permute-start | bytes 368 | tf_op jit(solution)/shard_map/ppermute | solution.py:22
  425.9 6.7 %collective-permute-start.65 = (f32[1,4,18,1]{3,2,1,0:T(8,128)S(1)}, f32[1,4,18,1]{3,2,1,0:T(8,128)S(1)}, u32[]{:S(2)}, u32[]{:S(2)}) collective-permute-start(f32[1,4,18,1]{3,2,1,0:T(8,128)S(1)} %get-tuple-element.94), channel_id=1, source_target_pairs={{0,1},{1,2},{2,3},{3,4},{4,5},{5,6},{6,7},{7,8},{8,9},{9,10},{10,1... | collective-permute-start | bytes 872 | tf_op jit(solution)/shard_map/ppermute | solution.py:22
  478.5 7.2 %collective-permute-start.76 = (f32[1,6,34,1]{3,0,2,1:T(1,128)S(1)}, f32[1,6,34,1]{3,0,2,1:T(1,128)S(1)}, u32[]{:S(2)}, u32[]{:S(2)}) collective-permute-start(f32[1,6,34,1]{3,0,2,1:T(1,128)S(1)} %get-tuple-element.65), channel_id=1, source_target_pairs={{1,0},{2,1},{3,2},{4,3},{5,4},{6,5},{7,6},{8,7},{9,8},{10,9},{11,1... | collective-permute-start | bytes 2456 | tf_op jit(solution)/shard_map/ppermute | solution.py:24
  502.3 10.7 %collective-permute-start.82 = (f32[1,6,34,1]{3,0,2,1:T(1,128)S(1)}, f32[1,6,34,1]{3,0,2,1:T(1,128)S(1)}, u32[]{:S(2)}, u32[]{:S(2)}) collective-permute-start(f32[1,6,34,1]{3,0,2,1:T(1,128)S(1)} %get-tuple-element.61), channel_id=1, source_target_pairs={{1,0},{2,1},{3,2},{4,3},{5,4},{6,5},{7,6},{8,7},{9,8},{10,9},{11,1... | collective-permute-start | bytes 2456 | tf_op jit(solution)/shard_map/ppermute | solution.py:24
  505.7 8.7 %collective-permute-start.83 = (f32[1,6,34,1]{3,0,2,1:T(1,128)S(1)}, f32[1,6,34,1]{3,0,2,1:T(1,128)S(1)}, u32[]{:S(2)}, u32[]{:S(2)}) collective-permute-start(f32[1,6,34,1]{3,0,2,1:T(1,128)S(1)} %get-tuple-element.62), channel_id=1, source_target_pairs={{0,1},{1,2},{2,3},{3,4},{4,5},{5,6},{6,7},{7,8},{8,9},{9,10},{10,1... | collective-permute-start | bytes 2456 | tf_op jit(solution)/shard_map/ppermute | solution.py:22
  546.9 12.8 %collective-permute-start.89 = (f32[1,10,66,1]{3,2,1,0:T(8,128)S(1)}, f32[1,10,66,1]{3,2,1,0:T(8,128)S(1)}, u32[]{:S(2)}, u32[]{:S(2)}) collective-permute-start(f32[1,10,66,1]{3,2,1,0:T(8,128)S(1)} %get-tuple-element.26), channel_id=1, source_target_pairs={{0,1},{1,2},{2,3},{3,4},{4,5},{5,6},{6,7},{7,8},{8,9},{9,10},{10,1... | collective-permute-start | bytes 7928 | tf_op jit(solution)/shard_map/ppermute | solution.py:22
  555.3 10.0 %collective-permute-start.88 = (f32[1,10,66,1]{3,2,1,0:T(8,128)S(1)}, f32[1,10,66,1]{3,2,1,0:T(8,128)S(1)}, u32[]{:S(2)}, u32[]{:S(2)}) collective-permute-start(f32[1,10,66,1]{3,2,1,0:T(8,128)S(1)} %get-tuple-element.25), channel_id=1, source_target_pairs={{1,0},{2,1},{3,2},{4,3},{5,4},{6,5},{7,6},{8,7},{9,8},{10,9},{11,1... | collective-permute-start | bytes 7928 | tf_op jit(solution)/shard_map/ppermute | solution.py:24
  578.4 8.9 %collective-permute-start.95 = (f32[1,10,66,1]{3,2,1,0:T(8,128)S(1)}, f32[1,10,66,1]{3,2,1,0:T(8,128)S(1)}, u32[]{:S(2)}, u32[]{:S(2)}) collective-permute-start(f32[1,10,66,1]{3,2,1,0:T(8,128)S(1)} %get-tuple-element.24), channel_id=1, source_target_pairs={{0,1},{1,2},{2,3},{3,4},{4,5},{5,6},{6,7},{7,8},{8,9},{9,10},{10,1... | collective-permute-start | bytes 7928 | tf_op jit(solution)/shard_map/ppermute | solution.py:22
  582.9 10.0 %collective-permute-start.94 = (f32[1,10,66,1]{3,2,1,0:T(8,128)S(1)}, f32[1,10,66,1]{3,2,1,0:T(8,128)S(1)}, u32[]{:S(2)}, u32[]{:S(2)}) collective-permute-start(f32[1,10,66,1]{3,2,1,0:T(8,128)S(1)} %get-tuple-element.23), channel_id=1, source_target_pairs={{1,0},{2,1},{3,2},{4,3},{5,4},{6,5},{7,6},{8,7},{9,8},{10,9},{11,1... | collective-permute-start | bytes 7928 | tf_op jit(solution)/shard_map/ppermute | solution.py:24
  605.9 9.0 %collective-permute-start.101 = (f32[1,10,66,1]{3,2,1,0:T(8,128)S(1)}, f32[1,10,66,1]{3,2,1,0:T(8,128)S(1)}, u32[]{:S(2)}, u32[]{:S(2)}) collective-permute-start(f32[1,10,66,1]{3,2,1,0:T(8,128)S(1)} %get-tuple-element.22), channel_id=1, source_target_pairs={{0,1},{1,2},{2,3},{3,4},{4,5},{5,6},{6,7},{7,8},{8,9},{9,10},{10,1... | collective-permute-start | bytes 7928 | tf_op jit(solution)/shard_map/ppermute | solution.py:22
  610.6 10.0 %collective-permute-start.100 = (f32[1,10,66,1]{3,2,1,0:T(8,128)S(1)}, f32[1,10,66,1]{3,2,1,0:T(8,128)S(1)}, u32[]{:S(2)}, u32[]{:S(2)}) collective-permute-start(f32[1,10,66,1]{3,2,1,0:T(8,128)S(1)} %get-tuple-element.21), channel_id=1, source_target_pairs={{1,0},{2,1},{3,2},{4,3},{5,4},{6,5},{7,6},{8,7},{9,8},{10,9},{11,1... | collective-permute-start | bytes 7928 | tf_op jit(solution)/shard_map/ppermute | solution.py:24
  (96 other events, 1566.0 us)
where the time goes:
time: 631 us; the launch traced here: 622 us
  starting transfers between devices  257 us (41%)
  waiting for transfers between devices  154 us (24%)
  local copies, waits for them, and re-layouts  134 us (21%)
  other arithmetic  74.7 us (12%)
    ppermute x51, starting transfers between devices, padded_2(): lax.ppermute(tail, axis, [(i, (i + 1) % count) for i in range(ends)])  136 us
    ppermute x51, starting transfers between devices, padded_2(): lax.ppermute(head, axis, [((i + 1) % count, i) for i in range(ends)])  121 us
    ppermute x51, waiting for transfers between devices, padded_2(): lax.ppermute(tail, axis, [(i, (i + 1) % count) for i in range(ends)])  96.8 us
    ppermute x51, waiting for transfers between devices, padded_2(): lax.ppermute(head, axis, [((i + 1) % count, i) for i in range(ends)])  57.1 us
    broadcast_in_dim x6, local copies, waits for them, and re-layouts, prolong(): wide = jnp.broadcast_to(wide, lead + (s[-3], 2, s[-2], 2, s[-1], 2))  24.2 us
    reduce_sum x9, other arithmetic, face_x(): return b.reshape(n0, n1 // 2, 2, n2 // 2, 2).sum(axis=(2, 4))  24.1 us
    reshape x2, local copies, waits for them, and re-layouts, blocks(): a.reshape(lead + (s[-3] // 2, 2, s[-2] // 2, 2, s[-1] // 2, 2))  22.4 us
    slice x10, local copies, waits for them, and re-layouts, face_x(): b = a[offset::2]  21.5 us
  transfers between devices with their start and end apart: 102, of which 50 were waited for; matrix products, arithmetic and copies ran while one was open for 20% of the time, Pallas kernels for 0%

commit v1 on v0

v1 whole, which is shorter than its diff:
```python
import functools

import jax
import jax.numpy as jnp
from jax import lax
from jax.experimental import pallas as pl
from jax.experimental.pallas import tpu as pltpu
from jax.sharding import PartitionSpec as P

MESH = pl.DeviceIdType.MESH
F32 = jnp.float32
W = 2.0 / 3.0
THIRD = 1.0 / 3.0
HI = lax.Precision.HIGHEST


def lanes(shape):
    return lax.broadcasted_iota(jnp.int32, shape, len(shape) - 1)


def roll(v, shift):
    return pltpu.roll(v, shift, 1)


def loop(count, body, init=0):
    return lax.fori_loop(0, count, body, init, unroll=True)


def each(count, body):
    def step(i, carry):
        body(i)
        return carry

    lax.fori_loop(0, count, step, 0, unroll=True)


def maps():
    row = lax.broadcasted_iota(jnp.int32, (128, 128), 0)
    col = lax.broadcasted_iota(jnp.int32, (128, 128), 1)
    hit = col == 32 + row // 2
    both = jnp.where(hit, 1.0, 0.0).astype(F32)
    odd = jnp.where(hit & (row % 2 == 1), 1.0, 0.0).astype(F32)
    even = jnp.where(hit & (row % 2 == 0), 1.0, 0.0).astype(F32)
    back = jnp.where(row == 32 + col // 2, 1.0, 0.0).astype(F32)
    return both, odd, even, back


def mm(a, b):
    return lax.dot(a, b, precision=HI, preferred_element_type=F32)


def kernel(
    ph_h, de_h, rh_h, os_h, or_h,
    ph, de, f0, rp, u0, fx, fy, fzu, fzd, w0, d0,
    rys, ryr, rzs, rzr, ys0, yr0, zs0, zr0,
    u1, f1, fx1, fy1u, fy1d, fz1u, fz1d, w1, d1,
    ys1, yr1, zs1, zr1,
    mb, mo, me, mt, t0, t1, t2,
    cc, gg,
    f2, u2, fx2, fy2, fz2, w2, d2,
    f3, u3, fx3, fy3, fz3, w3,
    osol, ores,
    in_sem, out_sem, rss, rrs, s0s, r0s, s1s, r1s, csx, crx, csn, crn, gsx, grx, gsn, grn,
):
    gx, gy, gz = lax.axis_index("gx"), lax.axis_index("gy"), lax.axis_index("gz")
    nx, ny, nz = lax.axis_size("gx"), lax.axis_size("gy"), lax.axis_size("gz")
    near = [
        ({"gx": gx + 1}, gx < nx - 1, gx > 0),
        ({"gx": gx - 1}, gx > 0, gx < nx - 1),
        ({"gy": gy + 1}, gy < ny - 1, gy > 0),
        ({"gy": gy - 1}, gy > 0, gy < ny - 1),
        ({"gz": gz + 1}, gz < nz - 1, gz > 0),
        ({"gz": gz - 1}, gz > 0, gz < nz - 1),
    ]

    loads = [
        pltpu.make_async_copy(ph_h, ph, in_sem.at[0]),
        pltpu.make_async_copy(de_h, de, in_sem.at[1]),
        pltpu.make_async_copy(rh_h.at[0], f0, in_sem.at[2]),
    ]
    for c in loads:
        c.start()

    for b in range(2):
        for x in (0, 9):
            u0[b, x, 8:72, :] = jnp.zeros((64, 128), F32)
        for x in (0, 5):
            u1[b, x, 8:40, :] = jnp.zeros((32, 128), F32)
        for ref in (yr0, zr0, yr1, zr1):
            for s in range(2):
                ref[b, s] = jnp.zeros((8, 128), F32)

    @pl.when((gy == 0) | (gy == ny - 1) | (gz == 0) | (gz == nz - 1))
    def _():
        for z in range(3):
            for y in range(3):
                if (z, y) != (1, 1):
                    cc[z, y] = jnp.zeros(cc.shape[2:], F32)
                    gg[z, y] = jnp.zeros(gg.shape[2:], F32)

    barrier = pltpu.get_barrier_semaphore()
    for d in range(1, 4):
        pl.semaphore_signal(barrier, inc=1, device_id={"gx": lax.rem(gx + d, nx)}, device_id_type=MESH)
    for where, ok, _ in near[2:]:
        @pl.when(ok)
        def _(where=where):
            pl.semaphore_signal(barrier, inc=1, device_id=where, device_id_type=MESH)
    arrivals = 3 + sum(jnp.where(ok, 1, 0) for _, ok, _ in near[2:])

    def faces(buf, n, rows, ys, yr, zs, zr, ss, rs):
        body = pl.ds(8, rows)
        pairs = [
            (buf.at[n, body], buf.at[0, body]),
            (buf.at[1, body], buf.at[n + 1, body]),
            (ys.at[1], yr.at[0]),
            (ys.at[0], yr.at[1]),
            (zs.at[1], zr.at[0]),
            (zs.at[0], zr.at[1]),
        ]

        def copy(d):
            src, dst = pairs[d]
            return pltpu.make_async_remote_copy(
                src_ref=src, dst_ref=dst, send_sem=ss.at[d], recv_sem=rs.at[d],
                device_id=near[d][0], device_id_type=MESH,
            )

        def start():
            for d in range(6):
                @pl.when(near[d][1])
                def _(d=d):
                    copy(d).start()

        def wait():
            for d in range(6):
                @pl.when(near[d][1])
                def _(d=d):
                    copy(d).wait_send()

                @pl.when(near[d][2])
                def _(d=d):
                    copy(d).wait_recv()

        return start, wait

    lane8 = lanes((8, 128))
    lane64 = lanes((64, 128))
    lane32 = lanes((32, 128))

    zero8 = jnp.zeros((8, 128), F32)

    def pack0(carry, plane, x):
        lo, hi = carry
        for t in range(8):
            v = plane[8 * t : 8 * t + 8]
            k = x * 8 + t
            here = lane8 == k
            lo = jnp.where(here, roll(v, k), lo)
            hi = jnp.where(here, roll(v, k + 1), hi)
        return lo, hi

    def z_beside0(plane, x, lo, hi):
        right = jnp.concatenate([roll(hi, 127 - (x * 8 + t)) for t in range(8)], axis=0)
        left = jnp.concatenate([roll(lo, lax.rem(128 - (x * 8 + t), 128)) for t in range(8)], axis=0)
        return (
            jnp.where(lane64 == 127, right, roll(plane, 127)),
            jnp.where(lane64 == 0, left, roll(plane, 1)),
        )

    def keep0(buf, ys, x, plane):
        buf[x + 1, 8:72, :] = plane
        ys[0, pl.ds(x, 1), :] = plane[0:1]
        ys[1, pl.ds(x, 1), :] = plane[63:64]

    def y_in(buf, yr, n, rows):
        def body(x):
            buf[x + 1, 7:8, :] = yr[0, pl.ds(x, 1), :]
            buf[x + 1, 8 + rows : 9 + rows, :] = yr[1, pl.ds(x, 1), :]

        each(n, body)

    def beside0(buf, x, lo, hi):
        c = buf[x + 1, 8:72, :]
        up, down = z_beside0(c, x, lo, hi)
        s = fx[x + 1] * buf[x + 2, 8:72, :] + fx[x] * buf[x, 8:72, :]
        s = s + fy[x, 8:72, :] * buf[x + 1, 9:73, :] + fy[x, 7:71, :] * buf[x + 1, 7:71, :]
        s = s + fzu[x] * up + fzd[x] * down
        return c, s

    def sweep0(src, dst, zr, ys, zs, out):
        lo, hi = zr[0], zr[1]

        def body(x, carry):
            c, s = beside0(src, x, lo, hi)
            new = c * THIRD + w0[x] * (f0[x] + s)
            keep0(dst, ys, x, new)
            if out:
                osol[x] = d0[x] * new
            return pack0(carry, new, x)

        packed = loop(8, body, (zero8, zero8))
        zs[0] = packed[0]
        zs[1] = packed[1]

    for c in loads[:2]:
        c.wait()

    def body(x, carry):
        plane = jnp.where(ph[x] == 1, 1000.0, 1.0).astype(F32) * de[x]
        keep0(rp, rys, x, plane)
        return pack0(carry, plane, x)

    packed = loop(8, body, (zero8, zero8))
    rzs[0] = packed[0]
    rzs[1] = packed[1]

    pl.semaphore_wait(barrier, arrivals)
    start, wait = faces(rp, 8, 64, rys, ryr, rzs, rzr, rss, rrs)
    start()
    both, odd, even, back = maps()
    mb[...] = both
    mo[...] = odd
    me[...] = even
    mt[...] = back
    loads[2].wait()
    wait()

    @pl.when(gx == 0)
    def _():
        rp[0, 8:72, :] = rp[1, 8:72, :]

    @pl.when(gx == nx - 1)
    def _():
        rp[9, 8:72, :] = rp[8, 8:72, :]

    for ok, got, own, s in ((gy == 0, ryr, rys, 0), (gy == ny - 1, ryr, rys, 1), (gz == 0, rzr, rzs, 0), (gz == nz - 1, rzr, rzs, 1)):
        @pl.when(ok)
        def _(got=got, own=own, s=s):
            got[s] = own[s]

    y_in(rp, ryr, 8, 64)
    lo, hi = rzr[0], rzr[1]
    fx[0] = 2.0 / (rp[0, 8:72, :] + rp[1, 8:72, :])

    def body(x, carry):
        c = rp[x + 1, 8:72, :]
        up, down = z_beside0(c, x, lo, hi)
        xu = 2.0 / (c + rp[x + 2, 8:72, :])
        yu = 2.0 / (c + rp[x + 1, 9:73, :])
        zu = 2.0 / (c + up)
        zd = 2.0 / (c + down)
        fx[x + 1] = xu
        fy[x, 8:72, :] = yu
        fy[x, 7:8, :] = 2.0 / (c[0:1] + rp[x + 1, 7:8, :])
        fzu[x] = zu
        fzd[x] = zd
        diag = xu + fx[x] + yu + fy[x, 7:71, :] + zu + zd
        d0[x] = diag
        w = W / diag
        w0[x] = w
        first = w * f0[x]
        keep0(u0.at[0], ys0.at[0], x, first)
        return pack0(carry, first, x)

    packed = loop(8, body, (zero8, zero8))
    zs0[0, 0] = packed[0]
    zs0[0, 1] = packed[1]

    def round0(b):
        return faces(u0.at[b], 8, 64, ys0.at[b], yr0.at[b], zs0.at[b], zr0.at[b], s0s.at[b], r0s.at[b])

    def round1(b):
        return faces(u1.at[b], 4, 32, ys1.at[b], yr1.at[b], zs1.at[b], zr1.at[b], s1s.at[b], r1s.at[b])

    start, wait = round0(0)
    start()

    own1 = (lane32 >= 32) & (lane32 < 96)

    def rows_of(ref, base, n, off):
        return ref[pl.ds(base + off, n, stride=2), :]

    def pair_rows(ref, base, n):
        return rows_of(ref, base, n, 0) + rows_of(ref, base, n, 1)

    for i in range(5):
        t0[0:64, :] = fx[2 * i]
        fx1[i] = mm(pair_rows(t0, 0, 32), mb[...])

    def body(i):
        yu = fy[2 * i, pl.ds(9, 32, stride=2), :] + fy[2 * i + 1, pl.ds(9, 32, stride=2), :]
        yd = fy[2 * i, pl.ds(7, 32, stride=2), :] + fy[2 * i + 1, pl.ds(7, 32, stride=2), :]
        t1[i, 0] = fzu[2 * i] + fzu[2 * i + 1]
        t1[i, 1] = fzd[2 * i] + fzd[2 * i + 1]
        zu = t1[i, 0, pl.ds(0, 32, stride=2), :] + t1[i, 0, pl.ds(1, 32, stride=2), :]
        zd = t1[i, 1, pl.ds(0, 32, stride=2), :] + t1[i, 1, pl.ds(1, 32, stride=2), :]
        yu, yd, zu, zd = mm(yu, mb[...]), mm(yd, mb[...]), mm(zu, mo[...]), mm(zd, me[...])
        fy1u[i] = yu
        fy1d[i] = yd
        fz1u[i] = zu
        fz1d[i] = zd
        diag = fx1[i] + fx1[i + 1] + yu + yd + zu + zd
        d1[i] = diag
        w1[i] = jnp.where(own1, W / jnp.where(own1, diag, 1.0), 0.0)

    each(4, body)

    def pack2(planes):
        out = zero8
        for x in range(2):
            for t in range(2):
                g = 2 * x + t
                v = roll(planes[x][8 * t : 8 * t + 8], (32 * g - 48) % 128)
                out = jnp.where((lane8 >= 32 * g) & (lane8 < 32 * g + 32), v, out)
        return out

    xu, yu, zu, dg = [], [], [], []
    for i in range(2):
        t0[0:32, :] = fx1[2 * i]
        t0[32:64, :] = fx1[2 * i + 2]
        t0[64:96, :] = fz1u[2 * i] + fz1u[2 * i + 1]
        t0[96:128, :] = fz1d[2 * i] + fz1d[2 * i + 1]
        t0[128:160, :] = fy1u[2 * i] + fy1u[2 * i + 1]
        t0[160:192, :] = fy1d[2 * i] + fy1d[2 * i + 1]
        xd_, xu_ = mm(pair_rows(t0, 0, 16), mb[...]), mm(pair_rows(t0, 32, 16), mb[...])
        zu_, zd_ = mm(pair_rows(t0, 64, 16), mo[...]), mm(pair_rows(t0, 96, 16), me[...])
        yu_, yd_ = mm(rows_of(t0, 128, 16, 1), mb[...]), mm(rows_of(t0, 160, 16, 0), mb[...])
        xu.append(xu_)
        yu.append(yu_)
        zu.append(zu_)
        dg.append(xu_ + xd_ + yu_ + yd_ + zu_ + zd_)
    for a, planes in enumerate((dg, xu, yu, zu)):
        cc[1, 1, gx, a] = pack2(planes)

    def gather(buf, sx, rx, sn, rn):
        def xcopy(d):
            return pltpu.make_async_remote_copy(
                src_ref=buf.at[1, 1, gx], dst_ref=buf.at[1, 1, gx], send_sem=sx.at[d - 1], recv_sem=rx.at[d - 1],
                device_id={"gx": lax.rem(gx + d, nx)}, device_id_type=MESH,
            )

        def ncopy(d):
            src = buf.at[1, 1] if d < 4 else buf.at[1]
            dst = [buf.at[1, 0], buf.at[1, 2], buf.at[0], buf.at[2]][d - 2]
            return pltpu.make_async_remote_copy(
                src_ref=src, dst_ref=dst, send_sem=sn.at[d - 2], recv_sem=rn.at[d - 2],
                device_id=near[d][0], device_id_type=MESH,
            )

        def xstart():
            for d in range(1, 4):
                xcopy(d).start()

        def xwait():
            for d in range(1, 4):
                pltpu.make_async_remote_copy(
                    src_ref=buf.at[1, 1, gx], dst_ref=buf.at[1, 1, lax.rem(gx + 4 - d, nx)],
                    send_sem=sx.at[d - 1], recv_sem=rx.at[d - 1],
                    device_id={"gx": lax.rem(gx + d, nx)}, device_id_type=MESH,
                ).wait()

        def nstart(ds):
            for d in ds:
                @pl.when(near[d][1])
                def _(d=d):
                    ncopy(d).start()

        def nwait(ds):
            for d in ds:
                @pl.when(near[d][1])
                def _(d=d):
                    ncopy(d).wait_send()

                @pl.when(near[d][2])
                def _(d=d):
                    ncopy(d).wait_recv()

        return (
            xstart, xwait,
            lambda: nstart((2, 3)), lambda: nwait((2, 3)),
            lambda: nstart((4, 5)), lambda: nwait((4, 5)),
        )

    cg = gather(cc, csx, crx, csn, crn)
    cg[0]()

    wait()
    y_in(u0.at[0], yr0.at[0], 8, 64)
    sweep0(u0.at[0], u0.at[1], zr0.at[0], ys0.at[1], zs0.at[1], False)
    start, wait = round0(1)
    start()
    cg[1]()
    cg[2]()
    wait()
    y_in(u0.at[1], yr0.at[1], 8, 64)

    lo, hi = zr0[1, 0], zr0[1, 1]

    def body(i):
        total = None
        for j in range(2):
            x = 2 * i + j
            c, s = beside0(u0.at[1], x, lo, hi)
            r = f0[x] - d0[x] * c + s
            total = r if total is None else total + r
        t1[i, 0] = total
        f1[i] = mm(t1[i, 0, pl.ds(0, 32, stride=2), :] + t1[i, 0, pl.ds(1, 32, stride=2), :], mb[...])

    each(4, body)

    def pack1(carry, plane, x):
        lo, hi = carry
        for t in range(4):
            v = plane[8 * t : 8 * t + 8]
            k = x * 4 + t
            here = lane8 // 8 == k
            lo = jnp.where(here, roll(v, lax.rem(8 * k + 96, 128)), lo)
            hi = jnp.where(here, roll(v, lax.rem(8 * k + 40, 128)), hi)
        return lo, hi

    def z_in1(plane, x, lo, hi):
        right = jnp.concatenate([roll(hi, lax.rem(96 + 128 - 8 * (x * 4 + t), 128)) for t in range(4)], axis=0)
        left = jnp.concatenate([roll(lo, lax.rem(24 + 128 - 8 * (x * 4 + t), 128)) for t in range(4)], axis=0)
        return jnp.where(lane32 >= 96, right, jnp.where(lane32 < 32, left, plane))

    def keep1(buf, ys, x, plane):
        buf[x + 1, 8:40, :] = plane
        ys[0, pl.ds(x, 1), :] = plane[0:1]
        ys[1, pl.ds(x, 1), :] = plane[31:32]

    def beside1(buf, x, lo, hi):
        c = buf[x + 1, 8:40, :]
        wide = z_in1(c, x, lo, hi)
        s = fx1[x + 1] * buf[x + 2, 8:40, :] + fx1[x] * buf[x, 8:40, :]
        s = s + fy1u[x] * buf[x + 1, 9:41, :] + fy1d[x] * buf[x + 1, 7:39, :]
        s = s + fz1u[x] * roll(wide, 127) + fz1d[x] * roll(wide, 1)
        return c, s

    def sweep1(src, dst, zr, ys, zs):
        lo, hi = zr[0], zr[1]

        def body(x, carry):
            c, s = beside1(src, x, lo, hi)
            new = c * THIRD + w1[x] * (f1[x] + s)
            keep1(dst, ys, x, new)
            return pack1(carry, new, x)

        packed = loop(4, body, (zero8, zero8))
        zs[0] = packed[0]
        zs[1] = packed[1]

    def body(x, carry):
        new = w1[x] * f1[x]
        keep1(u1.at[0], ys1.at[0], x, new)
        return pack1(carry, new, x)

    packed = loop(4, body, (zero8, zero8))
    zs1[0, 0] = packed[0]
    zs1[0, 1] = packed[1]
    start, wait = round1(0)
    start()
    cg[3]()
    cg[4]()
    wait()
    y_in(u1.at[0], yr1.at[0], 4, 32)
    sweep1(u1.at[0], u1.at[1], zr1.at[0], ys1.at[1], zs1.at[1])
    start, wait = round1(1)
    start()
    wait()
    y_in(u1.at[1], yr1.at[1], 4, 32)
    lo, hi = zr1[1, 0], zr1[1, 1]

    src2 = []
    for i in range(2):
        total = None
        for j in range(2):
            x = 2 * i + j
            c, s = beside1(u1.at[1], x, lo, hi)
            r = f1[x] - d1[x] * c + s
            total = r if total is None else total + r
        t0[32 * i : 32 * i + 32, :] = jnp.where(own1, total, 0.0)
        src2.append(mm(pair_rows(t0, 32 * i, 16), mb[...]))
    gg[1, 1, gx] = pack2(src2)
    fg = gather(gg, gsx, grx, gsn, grn)
    fg[0]()
    cg[5]()

    def spread2(get, put):
        def body(b):
            for y in range(3):
                v = [get(z, y, b) for z in range(3)]
                for x in range(2):
                    for t in range(2):
                        g = 2 * x + t
                        left = roll(v[0], (16 - 32 * g) % 128)
                        mid = roll(v[1], (48 - 32 * g) % 128)
                        right = roll(v[2], (80 - 32 * g) % 128)
                        out = jnp.where(lane8 < 48, left, jnp.where(lane8 < 80, mid, right))
                        out = jnp.where((lane8 >= 16) & (lane8 < 112), out, 0.0)
                        put(2 * b + x, 16 * y + 8 * t, out)

        each(4, body)

    def put_d(p, r, v):
        d2[p, r : r + 8, :] = v
        ok = v > 0.0
        w2[p, r : r + 8, :] = jnp.where(ok, W / jnp.where(ok, v, 1.0), 0.0)

    def put_x(p, r, v):
        fx2[p + 1, r : r + 8, :] = v

    def put_y(p, r, v):
        fy2[p, 8 + r : 16 + r, :] = v

    def put_z(p, r, v):
        fz2[p, r : r + 8, :] = v

    def put_f(p, r, v):
        f2[p, r : r + 8, :] = v
        u2[0, p + 1, 8 + r : 16 + r, :] = w2[p, r : r + 8, :] * v

    for a, put in enumerate((put_d, put_x, put_y, put_z)):
        spread2(lambda z, y, b, a=a: cc[z, y, b, a], put)
    fx2[0] = jnp.zeros((48, 128), F32)
    fx3[0] = jnp.zeros((24, 128), F32)

    def zero_rows(ref, n, rows):
        def body(p):
            ref[p, 0:8, :] = zero8
            ref[p, 8 + rows : 16 + rows, :] = zero8

        each(n, body)

    zero_rows(fy2, 8, 48)
    zero_rows(fy3, 4, 24)
    for b in range(2):
        zero_rows(u2.at[b], 10, 48)
        zero_rows(u3.at[b], 6, 24)
        for p in (0, 9):
            u2[b, p, 8:56, :] = jnp.zeros((48, 128), F32)
        for p in (0, 5):
            u3[b, p, 8:32, :] = jnp.zeros((24, 128), F32)

    lane48 = lanes((48, 128))
    row48 = lax.broadcasted_iota(jnp.int32, (48, 128), 0)

    def body(p):
        a, b = 2 * p, 2 * p + 1
        t2[p, 0] = fx2[b + 1]
        t2[p, 1] = fz2[a] + fz2[b]
        ysum = fy2[a, 8:56, :] + fy2[b, 8:56, :]
        t2[p, 2] = ysum
        inner = fx2[a + 1]
        inner = inner + jnp.where(row48 % 2 == 0, ysum, 0.0)
        inner = inner + jnp.where(lane48 % 2 == 0, fz2[a] + fz2[b], 0.0)
        t2[p, 3] = d2[a] + d2[b] - 2.0 * inner
        pick = lambda q, off: t2[p, q, pl.ds(off, 24, stride=2), :]
        fx3[p + 1] = mm(pick(0, 0) + pick(0, 1), mb[...])
        fz3[p] = mm(pick(1, 0) + pick(1, 1), mo[...])
        fy3[p, 8:32, :] = mm(pick(2, 1), mb[...])
        diag = mm(pick(3, 0) + pick(3, 1), mb[...])
        ok = diag > 0.0
        w3[p] = jnp.where(ok, W / jnp.where(ok, diag, 1.0), 0.0)

    each(4, body)

    fg[1]()
    fg[2]()
    fg[3]()
    fg[4]()
    fg[5]()
    spread2(lambda z, y, b: gg[z, y, b], put_f)

    def beside(buf, fxr, fyr, fzr, p, rows):
        c = buf[p + 1, 8 : 8 + rows, :]
        s = fxr[p + 1] * buf[p + 2, 8 : 8 + rows, :] + fxr[p] * buf[p, 8 : 8 + rows, :]
        s = s + fyr[p, 8 : 8 + rows, :] * buf[p + 1, 9 : 9 + rows, :]
        s = s + fyr[p, 7 : 7 + rows, :] * buf[p + 1, 7 : 7 + rows, :]
        z = fzr[p]
        return c, s + z * roll(c, 127) + roll(z * c, 1)

    def sweep2(src, dst):
        def body(p):
            c, s = beside(u2.at[src], fx2, fy2, fz2, p, 48)
            u2[dst, p + 1, 8:56, :] = c * THIRD + w2[p] * (f2[p] + s)

        each(8, body)

    def sweep3(src, dst):
        def body(p):
            c, s = beside(u3.at[src], fx3, fy3, fz3, p, 24)
            u3[dst, p + 1, 8:32, :] = c * THIRD + w3[p] * (f3[p] + s)

        each(4, body)

    sweep2(0, 1)

    def body(p):
        total = None
        for j in range(2):
            c, s = beside(u2.at[1], fx2, fy2, fz2, 2 * p + j, 48)
            r = f2[2 * p + j] - d2[2 * p + j] * c + s
            total = r if total is None else total + r
        t2[p, 0] = total
        src = mm(t2[p, 0, pl.ds(0, 24, stride=2), :] + t2[p, 0, pl.ds(1, 24, stride=2), :], mb[...])
        f3[p] = src
        u3[0, p + 1, 8:32, :] = w3[p] * src

    each(4, body)
    sweep3(0, 1)
    sweep3(1, 0)
    sweep3(0, 1)

    def body(p):
        e = mm(u3[1, p + 1, 8:32, :], mt[...])
        t2[p, 1, pl.ds(0, 24, stride=2), :] = e
        t2[p, 1, pl.ds(1, 24, stride=2), :] = e
        wide = t2[p, 1]
        for j in range(2):
            q = 2 * p + j
            u2[0, q + 1, 8:56, :] = u2[1, q + 1, 8:56, :] + jnp.where(d2[q] > 0.0, wide, 0.0)

    each(4, body)
    sweep2(0, 1)
    sweep2(1, 0)

    corr = []
    for i in range(2):
        e = mm(u2[0, 2 * gx + 1 + i, 24:40, :], mt[...])
        t0[pl.ds(32 * i, 16, stride=2), :] = e
        t0[pl.ds(32 * i + 1, 16, stride=2), :] = e
        corr.append(jnp.where(own1, t0[32 * i : 32 * i + 32, :], 0.0))
    carry = (zero8, zero8)
    for x in range(4):
        new = u1[1, x + 1, 8:40, :] + corr[x // 2]
        keep1(u1.at[0], ys1.at[0], x, new)
        carry = pack1(carry, new, x)
    zs1[0, 0] = carry[0]
    zs1[0, 1] = carry[1]
    for b in range(2):
        start, wait = round1(b)
        start()
        wait()
        y_in(u1.at[b], yr1.at[b], 4, 32)
        sweep1(u1.at[b], u1.at[1 - b], zr1.at[b], ys1.at[1 - b], zs1.at[1 - b])

    def body(i, carry):
        e = mm(u1[0, i + 1, 8:40, :], mt[...])
        t1[i, 0, pl.ds(0, 32, stride=2), :] = e
        t1[i, 0, pl.ds(1, 32, stride=2), :] = e
        wide = t1[i, 0]
        for j in range(2):
            x = 2 * i + j
            new = u0[1, x + 1, 8:72, :] + wide
            keep0(u0.at[0], ys0.at[0], x, new)
            carry = pack0(carry, new, x)
        return carry

    packed = loop(4, body, (zero8, zero8))
    zs0[0, 0] = packed[0]
    zs0[0, 1] = packed[1]
    for b in range(2):
        start, wait = round0(b)
        start()
        wait()
        y_in(u0.at[b], yr0.at[b], 8, 64)
        sweep0(u0.at[b], u0.at[1 - b], zr0.at[b], ys0.at[1 - b], zs0.at[1 - b], b == 1)

    start, wait = round0(0)
    start()
    out0 = pltpu.make_async_copy(osol, os_h.at[0], out_sem.at[0])
    out0.start()
    wait()
    y_in(u0.at[0], yr0.at[0], 8, 64)
    lo, hi = zr0[0, 0], zr0[0, 1]

    def body(x):
        c, s = beside0(u0.at[0], x, lo, hi)
        ores[x] = f0[x] - d0[x] * c + s

    each(8, body)
    out1 = pltpu.make_async_copy(ores, or_h.at[0], out_sem.at[1])
    out1.start()
    out0.wait()
    out1.wait()


def on_device(phase, density, rhs):
    V = lambda *s: pltpu.VMEM(s, F32)
    D = lambda *s: pltpu.SemaphoreType.DMA(s)
    scratch = [
        pltpu.VMEM((8, 64, 128), jnp.int32), V(8, 64, 128), V(8, 64, 128), V(10, 80, 128), V(2, 10, 80, 128),
        V(9, 64, 128), V(8, 80, 128), V(8, 64, 128), V(8, 64, 128), V(8, 64, 128), V(8, 64, 128),
        V(2, 8, 128), V(2, 8, 128), V(2, 8, 128), V(2, 8, 128),
        V(2, 2, 8, 128), V(2, 2, 8, 128), V(2, 2, 8, 128), V(2, 2, 8, 128),
        V(2, 6, 48, 128), V(4, 32, 128), V(5, 32, 128), V(4, 32, 128), V(4, 32, 128), V(4, 32, 128), V(4, 32, 128),
        V(4, 32, 128), V(4, 32, 128),
        V(2, 2, 8, 128), V(2, 2, 8, 128), V(2, 2, 8, 128), V(2, 2, 8, 128),
        V(128, 128), V(128, 128), V(128, 128), V(128, 128), V(256, 128), V(4, 2, 64, 128), V(4, 4, 48, 128),
        V(3, 3, 4, 4, 8, 128), V(3, 3, 4, 8, 128),
        V(8, 48, 128), V(2, 10, 64, 128), V(9, 48, 128), V(8, 64, 128), V(8, 48, 128), V(8, 48, 128), V(8, 48, 128),
        V(4, 24, 128), V(2, 6, 40, 128), V(5, 24, 128), V(4, 40, 128), V(4, 24, 128), V(4, 24, 128),
        V(8, 64, 128), V(8, 64, 128),
        D(3), D(2), D(6), D(6), D(2, 6), D(2, 6), D(2, 6), D(2, 6),
        D(3), D(3), D(4), D(4), D(3), D(3), D(4), D(4),
    ]
    shape = jax.ShapeDtypeStruct(rhs.shape, F32)
    return pl.pallas_call(
        kernel,
        out_shape=(shape, shape),
        in_specs=[pl.BlockSpec(memory_space=pl.ANY)] * 3,
        out_specs=(pl.BlockSpec(memory_space=pl.ANY),) * 2,
        scratch_shapes=scratch,
        compiler_params=pltpu.CompilerParams(collective_id=0, has_side_effects=True),
        name="vcycle",
    )(phase, density, rhs)


def solution(mesh):
    in_specs = (P("gx", "gy", "gz"), P("gx", "gy", "gz"), P(None, "gx", "gy", "gz"))
    out_specs = (P(None, "gx", "gy", "gz"), P(None, "gx", "gy", "gz"))
    return jax.shard_map(on_device, mesh=mesh, in_specs=in_specs, out_specs=out_specs, check_vma=False)
```

time: 631 us -> 56.1 us (0.09)
  the two profiles are of different devices: /device:TPU:127 before, /device:TPU:97 now
where the time goes in v1:
time: 56.1 us; the launch traced here: 56 us
  Pallas kernels  52.9 us (94%)
  local copies, waits for them, and re-layouts  2.42 us (4%)
  between operations  0.65 us (1%)
    pallas_call x1, Pallas kernels, on_device(): pl.pallas_call(kernel, out_shape=(shape, shape), in_specs=[pl.BlockSpec(m...  52.9 us
    unnamed x4, local copies, waits for them, and re-layouts  2.42 us

profile of v1, /device:TPU:97, one launch (start us, length us, event | category | flops | bytes accessed | tf_op | source)
XLA Modules:
  0.0 56.0 jit_solution(9747567502616632224)
XLA Ops:
  0.6 52.9 %vcycle.1 = (f32[1,8,64,128]{3,2,1,0:T(8,128)}, f32[1,8,64,128]{3,2,1,0:T(8,128)}) custom-call(s32[8,64,128]{2,1,0:T(8,128)} %ph_h.1, f32[8,64,128]{2,1,0:T(8,128)} %de_h.1, f32[1,8,64,128]{3,2,1,0:T(8,128)} %rh_h.1), custom_call_target="tpu_custom_call" | custom-call | tf_op jit(solution)/shard_map/vcycle/pallas_call | solution.py:708
  53.6 0.0 copy-start
  53.6 1.7 %copy.7 = f32[1,8,64,128]{3,2,1,0:T(8,128)} copy(f32[1,8,64,128]{3,2,1,0:T(8,128)} %get-tuple-element.4) | data formatting | bytes 524288
  55.3 0.0 copy-done
  55.3 0.7 %copy.8 = f32[1,8,64,128]{3,2,1,0:T(8,128)} copy(f32[1,8,64,128]{3,2,1,0:T(8,128)S(1)} %copy-done) | data formatting | bytes 524288
Async XLA Ops:
  53.6 1.7 %copy-start = (f32[1,8,64,128]{3,2,1,0:T(8,128)S(1)}, f32[1,8,64,128]{3,2,1,0:T(8,128)}, u32[]{:S(2)}) copy-start(f32[1,8,64,128]{3,2,1,0:T(8,128)} %get-tuple-element.5) | copy-start | bytes 786436

commit v2 on v1

--- a/solution.py
+++ b/solution.py
@@ -11,7 +11,7 @@
 F32 = jnp.float32
 W = 2.0 / 3.0
 THIRD = 1.0 / 3.0
-HI = lax.Precision.HIGHEST
+BF16 = jnp.bfloat16
 
 
 def lanes(shape):
@@ -38,29 +38,33 @@
     row = lax.broadcasted_iota(jnp.int32, (128, 128), 0)
     col = lax.broadcasted_iota(jnp.int32, (128, 128), 1)
     hit = col == 32 + row // 2
-    both = jnp.where(hit, 1.0, 0.0).astype(F32)
-    odd = jnp.where(hit & (row % 2 == 1), 1.0, 0.0).astype(F32)
-    even = jnp.where(hit & (row % 2 == 0), 1.0, 0.0).astype(F32)
-    back = jnp.where(row == 32 + col // 2, 1.0, 0.0).astype(F32)
-    return both, odd, even, back
+    both = jnp.where(hit, 1.0, 0.0)
+    odd = jnp.where(hit & (row % 2 == 1), 1.0, 0.0)
+    even = jnp.where(hit & (row % 2 == 0), 1.0, 0.0)
+    back = jnp.where(row == 32 + col // 2, 1.0, 0.0)
+    return [jnp.concatenate([m.astype(BF16)] * 3, axis=0) for m in (both, odd, even, back)]
 
 
 def mm(a, b):
-    return lax.dot(a, b, precision=HI, preferred_element_type=F32)
+    hi = a.astype(BF16)
+    rest = a - hi.astype(F32)
+    mid = rest.astype(BF16)
+    low = (rest - mid.astype(F32)).astype(BF16)
+    return lax.dot(jnp.concatenate([hi, mid, low], axis=1), b, preferred_element_type=F32)
 
 
 def kernel(
     ph_h, de_h, rh_h, os_h, or_h,
     ph, de, f0, rp, u0, fx, fy, fzu, fzd, w0, d0,
     rys, ryr, rzs, rzr, ys0, yr0, zs0, zr0,
-    u1, f1, fx1, fy1u, fy1d, fz1u, fz1d, w1, d1,
-    ys1, yr1, zs1, zr1,
-    mb, mo, me, mt, t0, t1, t2,
+    u1, f1, fx1, fy1u, fy1d, fz1u, fz1d, d1, w1, ce1,
+    pkc, zpc, rxc, ryc, rzc, pkf, zpf, rxf, ryf, rzf,
+    mb, mo, me, mt, t0, t1, t2, t3, t4, t5, f1e,
     cc, gg,
     f2, u2, fx2, fy2, fz2, w2, d2,
     f3, u3, fx3, fy3, fz3, w3,
     osol, ores,
-    in_sem, out_sem, rss, rrs, s0s, r0s, s1s, r1s, csx, crx, csn, crn, gsx, grx, gsn, grn,
+    in_sem, out_sem, rss, rrs, s0s, r0s, s1c, r1c, s1f, r1f, csx, crx, csn, crn, gs, gr,
 ):
     gx, gy, gz = lax.axis_index("gx"), lax.axis_index("gy"), lax.axis_index("gz")
     nx, ny, nz = lax.axis_size("gx"), lax.axis_size("gy"), lax.axis_size("gz")
@@ -81,31 +85,42 @@
     for c in loads:
         c.start()
 
-    for b in range(2):
+    for b in range(3):
         for x in (0, 9):
             u0[b, x, 8:72, :] = jnp.zeros((64, 128), F32)
-        for x in (0, 5):
-            u1[b, x, 8:40, :] = jnp.zeros((32, 128), F32)
-        for ref in (yr0, zr0, yr1, zr1):
+        for ref in (yr0, zr0):
             for s in range(2):
                 ref[b, s] = jnp.zeros((8, 128), F32)
 
-    @pl.when((gy == 0) | (gy == ny - 1) | (gz == 0) | (gz == nz - 1))
+    edge = (gx == 0) | (gx == nx - 1) | (gy == 0) | (gy == ny - 1) | (gz == 0) | (gz == nz - 1)
+
+    @pl.when(edge)
     def _():
-        for z in range(3):
-            for y in range(3):
-                if (z, y) != (1, 1):
-                    cc[z, y] = jnp.zeros(cc.shape[2:], F32)
-                    gg[z, y] = jnp.zeros(gg.shape[2:], F32)
-
+        for ref in (cc, gg, rxc, ryc, rzc, rxf, ryf, rzf):
+            ref[...] = jnp.zeros(ref.shape, F32)
+
+    def inside(at, step, count):
+        return (at >= 0) if step == 0 else (at < count - 1) if step > 0 else (at > 0)
+
+    def yz_ok(sy, sz):
+        return inside(gy, sy, ny) & inside(gz, sz, nz)
+
+    def at(sx, sy, sz):
+        return {"gx": sx, "gy": gy + sy, "gz": gz + sz}
+
+    steps = (-1, 0, 1)
     barrier = pltpu.get_barrier_semaphore()
-    for d in range(1, 4):
-        pl.semaphore_signal(barrier, inc=1, device_id={"gx": lax.rem(gx + d, nx)}, device_id_type=MESH)
-    for where, ok, _ in near[2:]:
-        @pl.when(ok)
-        def _(where=where):
-            pl.semaphore_signal(barrier, inc=1, device_id=where, device_id_type=MESH)
-    arrivals = 3 + sum(jnp.where(ok, 1, 0) for _, ok, _ in near[2:])
+    arrivals = 0
+    for sy in steps:
+        for sz in steps:
+            ok = yz_ok(sy, sz)
+            n = 3 if (sy, sz) == (0, 0) else 4
+            arrivals = arrivals + jnp.where(ok, n, 0)
+
+            @pl.when(ok)
+            def _(sy=sy, sz=sz, n=n):
+                for d in range(4 - n, 4):
+                    pl.semaphore_signal(barrier, inc=1, device_id=at(lax.rem(gx + d, nx), sy, sz), device_id_type=MESH)
 
     def faces(buf, n, rows, ys, yr, zs, zr, ss, rs):
         body = pl.ds(8, rows)
@@ -269,9 +284,70 @@
     def round0(b):
         return faces(u0.at[b], 8, 64, ys0.at[b], yr0.at[b], zs0.at[b], zr0.at[b], s0s.at[b], r0s.at[b])
 
-    def round1(b):
-        return faces(u1.at[b], 4, 32, ys1.at[b], yr1.at[b], zs1.at[b], zr1.at[b], s1s.at[b], r1s.at[b])
-
+    box = [(a, b, c) for a in steps for b in steps for c in steps if (a, b, c) != (0, 0, 0)]
+
+    def box_exchange(pk, zp, rx, ry, rz, ss, rs):
+        def copy(a, b, c):
+            if c:
+                src, dst = zp.at[(c + 1) // 2], rz.at[1 - a, 1 - b, (1 - c) // 2]
+            elif b:
+                src, dst = pk.at[:, :, pl.ds(24 if b > 0 else 0, 8)], ry.at[1 - a, (1 - b) // 2]
+            else:
+                src, dst = pk, rx.at[(1 - a) // 2]
+            return pltpu.make_async_remote_copy(
+                src_ref=src, dst_ref=dst, send_sem=ss.at[a + 1, b + 1, c + 1], recv_sem=rs.at[a + 1, b + 1, c + 1],
+                device_id=at(gx + a, b, c), device_id_type=MESH,
+            )
+
+        def start():
+            for a, b, c in sorted(box, key=lambda o: -sum(map(abs, o))):
+                @pl.when(inside(gx, a, nx) & yz_ok(b, c))
+                def _(a=a, b=b, c=c):
+                    copy(a, b, c).start()
+
+        def wait():
+            for a, b, c in box:
+                @pl.when(inside(gx, a, nx) & yz_ok(b, c))
+                def _(a=a, b=b, c=c):
+                    copy(a, b, c).wait_send()
+
+                @pl.when(inside(gx, -a, nx) & yz_ok(-b, -c))
+                def _(a=a, b=b, c=c):
+                    copy(a, b, c).wait_recv()
+
+        return start, wait
+
+    def pack_box(get, pk, zp, a):
+        planes = [get(x) for x in range(4)]
+        lo, hi = zero8, zero8
+        for i in range(2):
+            pk[a, i] = jnp.where(own1, planes[2 * i], roll(planes[2 * i + 1], 64))
+        for x in range(4):
+            for t in range(4):
+                v = planes[x][8 * t : 8 * t + 8]
+                k = x * 4 + t
+                here = lane8 // 8 == k
+                lo = jnp.where(here, roll(v, (8 * k + 96) % 128), lo)
+                hi = jnp.where(here, roll(v, (8 * k + 40) % 128), hi)
+        zp[0, a] = lo
+        zp[1, a] = hi
+
+    def unpack_box(own, rx, ry, rz, a, put):
+        for dx in range(3):
+            for x in range(4):
+                i = x // 2
+                turn = (lambda v: roll(v, 64)) if x % 2 else (lambda v: v)
+                mid = own(x) if dx == 1 else turn(rx[dx // 2, a, i])
+                centre = jnp.concatenate([turn(ry[dx, 0, a, i]), mid, turn(ry[dx, 1, a, i])], axis=0)
+                tiles = [(0, 3), (1, 0), (1, 1), (1, 2), (1, 3), (2, 0)]
+                left = jnp.concatenate([roll(rz[dx, dy, 0, a], (24 - 8 * (4 * x + t)) % 128) for dy, t in tiles], axis=0)
+                right = jnp.concatenate([roll(rz[dx, dy, 1, a], (96 - 8 * (4 * x + t)) % 128) for dy, t in tiles], axis=0)
+                out = jnp.where((lane48 >= 96) & (lane48 < 104), right, 0.0)
+                out = jnp.where((lane48 >= 32) & (lane48 < 96), centre, out)
+                out = jnp.where((lane48 >= 24) & (lane48 < 32), left, out)
+                put(4 * dx + x, out)
+
+    lane48 = lanes((48, 128))
     start, wait = round0(0)
     start()
 
@@ -300,10 +376,14 @@
         fz1u[i] = zu
         fz1d[i] = zd
         diag = fx1[i] + fx1[i + 1] + yu + yd + zu + zd
-        d1[i] = diag
-        w1[i] = jnp.where(own1, W / jnp.where(own1, diag, 1.0), 0.0)
+        d1[i] = jnp.where(own1, diag, 0.0)
 
     each(4, body)
+    parts1 = (lambda x: d1[x], lambda x: fx1[x + 1], lambda x: fy1u[x], lambda x: fz1u[x])
+    for a, get in enumerate(parts1):
+        pack_box(get, pkc, zpc, a)
+    c_start, c_wait = box_exchange(pkc, zpc, rxc, ryc, rzc, s1c, r1c)
+    c_start()
 
     def pack2(planes):
         out = zero8
@@ -408,81 +488,109 @@
 
     each(4, body)
 
-    def pack1(carry, plane, x):
-        lo, hi = carry
-        for t in range(4):
-            v = plane[8 * t : 8 * t + 8]
-            k = x * 4 + t
-            here = lane8 // 8 == k
-            lo = jnp.where(here, roll(v, lax.rem(8 * k + 96, 128)), lo)
-            hi = jnp.where(here, roll(v, lax.rem(8 * k + 40, 128)), hi)
-        return lo, hi
-
-    def z_in1(plane, x, lo, hi):
-        right = jnp.concatenate([roll(hi, lax.rem(96 + 128 - 8 * (x * 4 + t), 128)) for t in range(4)], axis=0)
-        left = jnp.concatenate([roll(lo, lax.rem(24 + 128 - 8 * (x * 4 + t), 128)) for t in range(4)], axis=0)
-        return jnp.where(lane32 >= 96, right, jnp.where(lane32 < 32, left, plane))
-
-    def keep1(buf, ys, x, plane):
-        buf[x + 1, 8:40, :] = plane
-        ys[0, pl.ds(x, 1), :] = plane[0:1]
-        ys[1, pl.ds(x, 1), :] = plane[31:32]
-
-    def beside1(buf, x, lo, hi):
-        c = buf[x + 1, 8:40, :]
-        wide = z_in1(c, x, lo, hi)
-        s = fx1[x + 1] * buf[x + 2, 8:40, :] + fx1[x] * buf[x, 8:40, :]
-        s = s + fy1u[x] * buf[x + 1, 9:41, :] + fy1d[x] * buf[x + 1, 7:39, :]
-        s = s + fz1u[x] * roll(wide, 127) + fz1d[x] * roll(wide, 1)
-        return c, s
-
-    def sweep1(src, dst, zr, ys, zs):
-        lo, hi = zr[0], zr[1]
-
-        def body(x, carry):
-            c, s = beside1(src, x, lo, hi)
-            new = c * THIRD + w1[x] * (f1[x] + s)
-            keep1(dst, ys, x, new)
-            return pack1(carry, new, x)
-
-        packed = loop(4, body, (zero8, zero8))
-        zs[0] = packed[0]
-        zs[1] = packed[1]
-
-    def body(x, carry):
-        new = w1[x] * f1[x]
-        keep1(u1.at[0], ys1.at[0], x, new)
-        return pack1(carry, new, x)
-
-    packed = loop(4, body, (zero8, zero8))
-    zs1[0, 0] = packed[0]
-    zs1[0, 1] = packed[1]
-    start, wait = round1(0)
-    start()
+    pack_box(lambda x: f1[x], pkf, zpf, 0)
+    f_start, f_wait = box_exchange(pkf, zpf, rxf, ryf, rzf, s1f, r1f)
+    f_start()
     cg[3]()
     cg[4]()
-    wait()
-    y_in(u1.at[0], yr1.at[0], 4, 32)
-    sweep1(u1.at[0], u1.at[1], zr1.at[0], ys1.at[1], zs1.at[1])
-    start, wait = round1(1)
-    start()
-    wait()
-    y_in(u1.at[1], yr1.at[1], 4, 32)
-    lo, hi = zr1[1, 0], zr1[1, 1]
+    c_wait()
+    for a, get in enumerate(parts1):
+        def put(p, out, a=a):
+            ce1[a, p, 8:56, :] = out
+            if a == 0:
+                ok = out > 0.0
+                w1[p] = jnp.where(ok, W / jnp.where(ok, out, 1.0), 0.0)
+
+        unpack_box(get, rxc, ryc, rzc, a, put)
+
+    def zero_rows(ref, n, rows):
+        def body(p):
+            ref[p, 0:8, :] = zero8
+            ref[p, 8 + rows : 16 + rows, :] = zero8
+
+        each(n, body)
+
+    zero_rows(ce1.at[2], 12, 48)
+    for b in range(2):
+        zero_rows(u1.at[b], 12, 48)
+    f_wait()
+
+    def put(p, out):
+        f1e[p] = out
+        u1[0, p, 8:56, :] = w1[p] * out
+
+    unpack_box(lambda x: f1[x], rxf, ryf, rzf, 0, put)
+
+    def beside1(buf, p, r0, n):
+        c = buf[p, r0 : r0 + n, :]
+        s = ce1[1, p, r0 : r0 + n, :] * buf[p + 1, r0 : r0 + n, :]
+        s = s + ce1[1, p - 1, r0 : r0 + n, :] * buf[p - 1, r0 : r0 + n, :]
+        s = s + ce1[2, p, r0 : r0 + n, :] * buf[p, r0 + 1 : r0 + 1 + n, :]
+        s = s + ce1[2, p, r0 - 1 : r0 - 1 + n, :] * buf[p, r0 - 1 : r0 - 1 + n, :]
+        z = ce1[3, p, r0 : r0 + n, :]
+        return c, s + z * roll(c, 127) + roll(z * c, 1)
+
+    def sweep1(src, dst, first, count):
+        def body(i):
+            p = i + first
+            c, s = beside1(u1.at[src], p, 8, 48)
+            u1[dst, p, 8:56, :] = c * THIRD + w1[p] * (f1e[p] + s)
+
+        each(count, body)
+
+    sweep1(0, 1, 1, 10)
 
     src2 = []
     for i in range(2):
         total = None
         for j in range(2):
             x = 2 * i + j
-            c, s = beside1(u1.at[1], x, lo, hi)
+            c, s = beside1(u1.at[1], x + 4, 16, 32)
             r = f1[x] - d1[x] * c + s
             total = r if total is None else total + r
         t0[32 * i : 32 * i + 32, :] = jnp.where(own1, total, 0.0)
         src2.append(mm(pair_rows(t0, 32 * i, 16), mb[...]))
     gg[1, 1, gx] = pack2(src2)
-    fg = gather(gg, gsx, grx, gsn, grn)
-    fg[0]()
+
+    def fcopy(d, sy, sz):
+        return pltpu.make_async_remote_copy(
+            src_ref=gg.at[1, 1, gx], dst_ref=gg.at[1 - sz, 1 - sy, gx],
+            send_sem=gs.at[d, sy + 1, sz + 1], recv_sem=gr.at[d, sy + 1, sz + 1],
+            device_id=at(lax.rem(gx + d, nx), sy, sz), device_id_type=MESH,
+        )
+
+    def fback(d, sy, sz):
+        return pltpu.make_async_remote_copy(
+            src_ref=gg.at[1, 1, gx], dst_ref=gg.at[1 - sz, 1 - sy, lax.rem(gx + 4 - d, nx)],
+            send_sem=gs.at[d, sy + 1, sz + 1], recv_sem=gr.at[d, sy + 1, sz + 1],
+            device_id=at(lax.rem(gx + d, nx), sy, sz), device_id_type=MESH,
+        )
+
+    order = sorted([(sy, sz) for sy in steps for sz in steps], key=lambda o: -abs(o[0]) - abs(o[1]))
+
+    def g_start():
+        for sy, sz in order:
+            @pl.when(yz_ok(sy, sz))
+            def _(sy=sy, sz=sz):
+                for d in (2, 1, 3, 0):
+                    if (d, sy, sz) != (0, 0, 0):
+                        fcopy(d, sy, sz).start()
+
+    def g_wait():
+        for sy, sz in order:
+            @pl.when(yz_ok(sy, sz))
+            def _(sy=sy, sz=sz):
+                for d in range(4):
+                    if (d, sy, sz) != (0, 0, 0):
+                        fcopy(d, sy, sz).wait_send()
+
+            @pl.when(yz_ok(-sy, -sz))
+            def _(sy=sy, sz=sz):
+                for d in range(4):
+                    if (d, sy, sz) != (0, 0, 0):
+                        fback(d, sy, sz).wait_recv()
+
+    g_start()
     cg[5]()
 
     def spread2(get, put):
@@ -517,44 +625,36 @@
 
     def put_f(p, r, v):
         f2[p, r : r + 8, :] = v
-        u2[0, p + 1, 8 + r : 16 + r, :] = w2[p, r : r + 8, :] * v
+        u2[0, p + 2, 8 + r : 16 + r, :] = w2[p, r : r + 8, :] * v
 
     for a, put in enumerate((put_d, put_x, put_y, put_z)):
         spread2(lambda z, y, b, a=a: cc[z, y, b, a], put)
     fx2[0] = jnp.zeros((48, 128), F32)
     fx3[0] = jnp.zeros((24, 128), F32)
 
-    def zero_rows(ref, n, rows):
-        def body(p):
-            ref[p, 0:8, :] = zero8
-            ref[p, 8 + rows : 16 + rows, :] = zero8
-
-        each(n, body)
-
     zero_rows(fy2, 8, 48)
     zero_rows(fy3, 4, 24)
     for b in range(2):
-        zero_rows(u2.at[b], 10, 48)
+        zero_rows(u2.at[b], 12, 48)
         zero_rows(u3.at[b], 6, 24)
-        for p in (0, 9):
+        for p in (0, 1, 10, 11):
             u2[b, p, 8:56, :] = jnp.zeros((48, 128), F32)
         for p in (0, 5):
             u3[b, p, 8:32, :] = jnp.zeros((24, 128), F32)
 
-    lane48 = lanes((48, 128))
     row48 = lax.broadcasted_iota(jnp.int32, (48, 128), 0)
 
     def body(p):
         a, b = 2 * p, 2 * p + 1
-        t2[p, 0] = fx2[b + 1]
-        t2[p, 1] = fz2[a] + fz2[b]
+        t5[p, 0] = fx2[b + 1]
+        t5[p, 1] = fz2[a] + fz2[b]
         ysum = fy2[a, 8:56, :] + fy2[b, 8:56, :]
-        t2[p, 2] = ysum
+        t5[p, 2] = ysum
         inner = fx2[a + 1]
         inner = inner + jnp.where(row48 % 2 == 0, ysum, 0.0)
         inner = inner + jnp.where(lane48 % 2 == 0, fz2[a] + fz2[b], 0.0)
-        t2[p, 3] = d2[a] + d2[b] - 2.0 * inner
-        pick = lambda q, off: t2[p, q, pl.ds(off, 24, stride=2), :]
+        t5[p, 3] = d2[a] + d2[b] - 2.0 * inner
+        pick = lambda q, off: t5[p, q, pl.ds(off, 24, stride=2), :]
         fx3[p + 1] = mm(pick(0, 0) + pick(0, 1), mb[...])
         fz3[p] = mm(pick(1, 0) + pick(1, 1), mo[...])
         fy3[p, 8:32, :] = mm(pick(2, 1), mb[...])
@@ -564,11 +664,7 @@
 
     each(4, body)
 
-    fg[1]()
-    fg[2]()
-    fg[3]()
-    fg[4]()
-    fg[5]()
+    g_wait()
     spread2(lambda z, y, b: gg[z, y, b], put_f)
 
     def beside(buf, fxr, fyr, fzr, p, rows):
@@ -581,8 +677,8 @@
 
     def sweep2(src, dst):
         def body(p):
-            c, s = beside(u2.at[src], fx2, fy2, fz2, p, 48)
-            u2[dst, p + 1, 8:56, :] = c * THIRD + w2[p] * (f2[p] + s)
+            c, s = beside(u2.at[src, pl.ds(1, 10)], fx2, fy2, fz2, p, 48)
+            u2[dst, p + 2, 8:56, :] = c * THIRD + w2[p] * (f2[p] + s)
 
         each(8, body)
 
@@ -598,11 +694,11 @@
     def body(p):
         total = None
         for j in range(2):
-            c, s = beside(u2.at[1], fx2, fy2, fz2, 2 * p + j, 48)
+            c, s = beside(u2.at[1, pl.ds(1, 10)], fx2, fy2, fz2, 2 * p + j, 48)
             r = f2[2 * p + j] - d2[2 * p + j] * c + s
             total = r if total is None else total + r
-        t2[p, 0] = total
-        src = mm(t2[p, 0, pl.ds(0, 24, stride=2), :] + t2[p, 0, pl.ds(1, 24, stride=2), :], mb[...])
+        t5[p, 0] = total
+        src = mm(t5[p, 0, pl.ds(0, 24, stride=2), :] + t5[p, 0, pl.ds(1, 24, stride=2), :], mb[...])
         f3[p] = src
         u3[0, p + 1, 8:32, :] = w3[p] * src
 
@@ -613,58 +709,67 @@
 
     def body(p):
         e = mm(u3[1, p + 1, 8:32, :], mt[...])
-        t2[p, 1, pl.ds(0, 24, stride=2), :] = e
-        t2[p, 1, pl.ds(1, 24, stride=2), :] = e
-        wide = t2[p, 1]
+        t5[p, 1, pl.ds(0, 24, stride=2), :] = e
+        t5[p, 1, pl.ds(1, 24, stride=2), :] = e
+        wide = t5[p, 1]
         for j in range(2):
             q = 2 * p + j
-            u2[0, q + 1, 8:56, :] = u2[1, q + 1, 8:56, :] + jnp.where(d2[q] > 0.0, wide, 0.0)
+            u2[0, q + 2, 8:56, :] = u2[1, q + 2, 8:56, :] + jnp.where(d2[q] > 0.0, wide, 0.0)
 
     each(4, body)
     sweep2(0, 1)
     sweep2(1, 0)
 
-    corr = []
-    for i in range(2):
-        e = mm(u2[0, 2 * gx + 1 + i, 24:40, :], mt[...])
-        t0[pl.ds(32 * i, 16, stride=2), :] = e
-        t0[pl.ds(32 * i + 1, 16, stride=2), :] = e
-        corr.append(jnp.where(own1, t0[32 * i : 32 * i + 32, :], 0.0))
-    carry = (zero8, zero8)
-    for x in range(4):
-        new = u1[1, x + 1, 8:40, :] + corr[x // 2]
-        keep1(u1.at[0], ys1.at[0], x, new)
-        carry = pack1(carry, new, x)
-    zs1[0, 0] = carry[0]
-    zs1[0, 1] = carry[1]
-    for b in range(2):
-        start, wait = round1(b)
-        start()
-        wait()
-        y_in(u1.at[b], yr1.at[b], 4, 32)
-        sweep1(u1.at[b], u1.at[1 - b], zr1.at[b], ys1.at[1 - b], zs1.at[1 - b])
-
-    def body(i, carry):
-        e = mm(u1[0, i + 1, 8:40, :], mt[...])
-        t1[i, 0, pl.ds(0, 32, stride=2), :] = e
-        t1[i, 0, pl.ds(1, 32, stride=2), :] = e
-        wide = t1[i, 0]
-        for j in range(2):
-            x = 2 * i + j
-            new = u0[1, x + 1, 8:72, :] + wide
-            keep0(u0.at[0], ys0.at[0], x, new)
-            carry = pack0(carry, new, x)
-        return carry
-
-    packed = loop(4, body, (zero8, zero8))
-    zs0[0, 0] = packed[0]
-    zs0[0, 1] = packed[1]
-    for b in range(2):
-        start, wait = round0(b)
-        start()
-        wait()
-        y_in(u0.at[b], yr0.at[b], 8, 64)
-        sweep0(u0.at[b], u0.at[1 - b], zr0.at[b], ys0.at[1 - b], zs0.at[1 - b], b == 1)
+    def body(q):
+        e = mm(u2[0, 2 * gx + q, 20:44, :], mt[...])
+        t2[q, pl.ds(0, 24, stride=2), :] = e
+        t2[q, pl.ds(1, 24, stride=2), :] = e
+
+    each(6, body)
+
+    def body(i):
+        p = i + 1
+        u1[0, p, 8:56, :] = u1[1, p, 8:56, :] + jnp.where(w1[p] > 0.0, t2[p // 2], 0.0)
+
+    each(10, body)
+    sweep1(0, 1, 2, 8)
+    sweep1(1, 0, 3, 6)
+
+    def body(q):
+        c = u1[0, q + 3, 12:52, :]
+        e = mm(c, mt[...])
+        t3[q, pl.ds(0, 40, stride=2), :] = e
+        t3[q, pl.ds(1, 40, stride=2), :] = e
+        t4[q, pl.ds(0, 40, stride=2), :] = c
+        t4[q, pl.ds(1, 40, stride=2), :] = c
+
+    each(6, body)
+
+    def body(p):
+        u0[0, p, :, :] = u0[1, p, :, :] + t3[(p + 1) // 2]
+
+    each(10, body)
+
+    def body(q, carry):
+        lo, hi = carry
+        for t in range(8):
+            v = t4[q + 1, 8 + 8 * t : 16 + 8 * t, :]
+            k = 16 * q + t
+            here = (lane8 == k) | (lane8 == k + 8)
+            a, b = roll(v, lax.rem(k + 97, 128)), roll(v, lax.rem(k + 32, 128))
+            lo = jnp.where(lane8 == k, a, jnp.where(lane8 == k + 8, roll(a, 8), lo))
+            hi = jnp.where(lane8 == k, b, jnp.where(lane8 == k + 8, roll(b, 8), hi))
+        return lo, hi
+
+    lo, hi = loop(4, body, (zero8, zero8))
+    zr0[0, 0] = zr0[1, 0] + lo
+    zr0[0, 1] = zr0[1, 1] + hi
+    sweep0(u0.at[0], u0.at[2], zr0.at[0], ys0.at[2], zs0.at[2], False)
+    start, wait = round0(2)
+    start()
+    wait()
+    y_in(u0.at[2], yr0.at[2], 8, 64)
+    sweep0(u0.at[2], u0.at[0], zr0.at[2], ys0.at[0], zs0.at[0], True)
 
     start, wait = round0(0)
     start()
@@ -687,22 +792,25 @@
 
 def on_device(phase, density, rhs):
     V = lambda *s: pltpu.VMEM(s, F32)
+    M = pltpu.VMEM((384, 128), BF16)
     D = lambda *s: pltpu.SemaphoreType.DMA(s)
     scratch = [
-        pltpu.VMEM((8, 64, 128), jnp.int32), V(8, 64, 128), V(8, 64, 128), V(10, 80, 128), V(2, 10, 80, 128),
+        pltpu.VMEM((8, 64, 128), jnp.int32), V(8, 64, 128), V(8, 64, 128), V(10, 80, 128), V(3, 10, 80, 128),
         V(9, 64, 128), V(8, 80, 128), V(8, 64, 128), V(8, 64, 128), V(8, 64, 128), V(8, 64, 128),
         V(2, 8, 128), V(2, 8, 128), V(2, 8, 128), V(2, 8, 128),
-        V(2, 2, 8, 128), V(2, 2, 8, 128), V(2, 2, 8, 128), V(2, 2, 8, 128),
-        V(2, 6, 48, 128), V(4, 32, 128), V(5, 32, 128), V(4, 32, 128), V(4, 32, 128), V(4, 32, 128), V(4, 32, 128),
-        V(4, 32, 128), V(4, 32, 128),
-        V(2, 2, 8, 128), V(2, 2, 8, 128), V(2, 2, 8, 128), V(2, 2, 8, 128),
-        V(128, 128), V(128, 128), V(128, 128), V(128, 128), V(256, 128), V(4, 2, 64, 128), V(4, 4, 48, 128),
+        V(3, 2, 8, 128), V(3, 2, 8, 128), V(3, 2, 8, 128), V(3, 2, 8, 128),
+        V(2, 12, 64, 128), V(4, 32, 128), V(5, 32, 128), V(4, 32, 128), V(4, 32, 128), V(4, 32, 128), V(4, 32, 128),
+        V(4, 32, 128), V(12, 48, 128), V(4, 12, 64, 128),
+        V(4, 2, 32, 128), V(2, 4, 8, 128), V(2, 4, 2, 32, 128), V(3, 2, 4, 2, 8, 128), V(3, 3, 2, 4, 8, 128),
+        V(1, 2, 32, 128), V(2, 1, 8, 128), V(2, 1, 2, 32, 128), V(3, 2, 1, 2, 8, 128), V(3, 3, 2, 1, 8, 128),
+        M, M, M, M, V(256, 128), V(4, 2, 64, 128), V(6, 48, 128), V(6, 80, 128), V(6, 80, 128), V(4, 4, 48, 128),
+        V(12, 48, 128),
         V(3, 3, 4, 4, 8, 128), V(3, 3, 4, 8, 128),
-        V(8, 48, 128), V(2, 10, 64, 128), V(9, 48, 128), V(8, 64, 128), V(8, 48, 128), V(8, 48, 128), V(8, 48, 128),
+        V(8, 48, 128), V(2, 12, 64, 128), V(9, 48, 128), V(8, 64, 128), V(8, 48, 128), V(8, 48, 128), V(8, 48, 128),
         V(4, 24, 128), V(2, 6, 40, 128), V(5, 24, 128), V(4, 40, 128), V(4, 24, 128), V(4, 24, 128),
         V(8, 64, 128), V(8, 64, 128),
-        D(3), D(2), D(6), D(6), D(2, 6), D(2, 6), D(2, 6), D(2, 6),
-        D(3), D(3), D(4), D(4), D(3), D(3), D(4), D(4),
+        D(3), D(2), D(6), D(6), D(3, 6), D(3, 6), D(3, 3, 3), D(3, 3, 3), D(3, 3, 3), D(3, 3, 3),
+        D(3), D(3), D(4), D(4), D(4, 3, 3), D(4, 3, 3),
     ]
     shape = jax.ShapeDtypeStruct(rhs.shape, F32)
     return pl.pallas_call(

time: 56.1 us -> 46.7 us (0.83)
  Pallas kernels: 52.9 us -> 43.6 us
    pallas_call x1, Pallas kernels: 52.9 us -> 43.6 us  [on_device(): pl.pallas_call(kernel, out_shape=(shape, shape), in_specs=[pl.BlockSpec(m...]
where the time goes in v2:
time: 46.7 us; the launch traced here: 46.6 us
  Pallas kernels  43.6 us (93%)
  local copies, waits for them, and re-layouts  2.42 us (5%)
  between operations  0.65 us (1%)
    pallas_call x1, Pallas kernels, on_device(): pl.pallas_call(kernel, out_shape=(shape, shape), in_specs=[pl.BlockSpec(m...  43.6 us
    unnamed x4, local copies, waits for them, and re-layouts  2.42 us

profile of v2, /device:TPU:97, one launch (start us, length us, event | category | flops | bytes accessed | tf_op | source)
XLA Modules:
  0.0 46.6 jit_solution(10985761280415747515)
XLA Ops:
  0.6 43.6 %vcycle.1 = (f32[1,8,64,128]{3,2,1,0:T(8,128)}, f32[1,8,64,128]{3,2,1,0:T(8,128)}) custom-call(s32[8,64,128]{2,1,0:T(8,128)} %ph_h.1, f32[8,64,128]{2,1,0:T(8,128)} %de_h.1, f32[1,8,64,128]{3,2,1,0:T(8,128)} %rh_h.1), custom_call_target="tpu_custom_call" | custom-call | tf_op jit(solution)/shard_map/vcycle/pallas_call | solution.py:816
  44.2 0.0 copy-start
  44.2 1.7 %copy.7 = f32[1,8,64,128]{3,2,1,0:T(8,128)} copy(f32[1,8,64,128]{3,2,1,0:T(8,128)} %get-tuple-element.4) | data formatting | bytes 524288
  45.9 0.0 copy-done
  45.9 0.7 %copy.8 = f32[1,8,64,128]{3,2,1,0:T(8,128)} copy(f32[1,8,64,128]{3,2,1,0:T(8,128)S(1)} %copy-done) | data formatting | bytes 524288
Async XLA Ops:
  44.2 1.7 %copy-start = (f32[1,8,64,128]{3,2,1,0:T(8,128)S(1)}, f32[1,8,64,128]{3,2,1,0:T(8,128)}, u32[]{:S(2)}) copy-start(f32[1,8,64,128]{3,2,1,0:T(8,128)} %get-tuple-element.5) | copy-start | bytes 786436

commit v3 on v2

--- a/solution.py
+++ b/solution.py
@@ -58,7 +58,7 @@
     ph, de, f0, rp, u0, fx, fy, fzu, fzd, w0, d0,
     rys, ryr, rzs, rzr, ys0, yr0, zs0, zr0,
     u1, f1, fx1, fy1u, fy1d, fz1u, fz1d, d1, w1, ce1,
-    pkc, zpc, rxc, ryc, rzc, pkf, zpf, rxf, ryf, rzf,
+    pkc, xyc, zpc, yzc, rxc, ryc, rzc, rec, pkf, xyf, zpf, yzf, rxf, ryf, rzf, ref_,
     mb, mo, me, mt, t0, t1, t2, t3, t4, t5, f1e,
     cc, gg,
     f2, u2, fx2, fy2, fz2, w2, d2,
@@ -85,19 +85,37 @@
     for c in loads:
         c.start()
 
+    edge = (gx == 0) | (gx == nx - 1) | (gy == 0) | (gy == ny - 1) | (gz == 0) | (gz == nz - 1)
+
+    @pl.when(edge)
+    def _():
+        for ref in (ryc, rzc, rec):
+            ref[...] = jnp.zeros(ref.shape, F32)
+
+    barrier = pltpu.get_barrier_semaphore()
+    arrivals = 0
+    for where, ok, back in near:
+        arrivals = arrivals + jnp.where(back, 1, 0)
+
+        @pl.when(ok)
+        def _(where=where):
+            pl.semaphore_signal(barrier, inc=1, device_id=where, device_id_type=MESH)
+
     for b in range(3):
         for x in (0, 9):
             u0[b, x, 8:72, :] = jnp.zeros((64, 128), F32)
         for ref in (yr0, zr0):
-            for s in range(2):
-                ref[b, s] = jnp.zeros((8, 128), F32)
-
-    edge = (gx == 0) | (gx == nx - 1) | (gy == 0) | (gy == ny - 1) | (gz == 0) | (gz == nz - 1)
+            for k in range(2):
+                ref[b, k] = jnp.zeros((8, 128), F32)
 
     @pl.when(edge)
     def _():
-        for ref in (cc, gg, rxc, ryc, rzc, rxf, ryf, rzf):
+        for ref in (gg, rxc, rxf, ryf, rzf, ref_):
             ref[...] = jnp.zeros(ref.shape, F32)
+        for z in range(3):
+            for y in range(3):
+                if (z, y) != (1, 1):
+                    cc[z, y] = jnp.zeros(cc.shape[2:], F32)
 
     def inside(at, step, count):
         return (at >= 0) if step == 0 else (at < count - 1) if step > 0 else (at > 0)
@@ -109,18 +127,6 @@
         return {"gx": sx, "gy": gy + sy, "gz": gz + sz}
 
     steps = (-1, 0, 1)
-    barrier = pltpu.get_barrier_semaphore()
-    arrivals = 0
-    for sy in steps:
-        for sz in steps:
-            ok = yz_ok(sy, sz)
-            n = 3 if (sy, sz) == (0, 0) else 4
-            arrivals = arrivals + jnp.where(ok, n, 0)
-
-            @pl.when(ok)
-            def _(sy=sy, sz=sz, n=n):
-                for d in range(4 - n, 4):
-                    pl.semaphore_signal(barrier, inc=1, device_id=at(lax.rem(gx + d, nx), sy, sz), device_id_type=MESH)
 
     def faces(buf, n, rows, ys, yr, zs, zr, ss, rs):
         body = pl.ds(8, rows)
@@ -286,12 +292,14 @@
 
     box = [(a, b, c) for a in steps for b in steps for c in steps if (a, b, c) != (0, 0, 0)]
 
-    def box_exchange(pk, zp, rx, ry, rz, ss, rs):
+    def box_exchange(pk, xy, zp, yz, rx, ry, rz, re, ss, rs):
         def copy(a, b, c):
-            if c:
-                src, dst = zp.at[(c + 1) // 2], rz.at[1 - a, 1 - b, (1 - c) // 2]
+            if b and c:
+                src, dst = yz.at[(b + 1) // 2, (c + 1) // 2], re.at[1 - a, (1 - b) // 2, (1 - c) // 2]
+            elif c:
+                src, dst = zp.at[(c + 1) // 2], rz.at[1 - a, (1 - c) // 2]
             elif b:
-                src, dst = pk.at[:, :, pl.ds(24 if b > 0 else 0, 8)], ry.at[1 - a, (1 - b) // 2]
+                src, dst = xy.at[(b + 1) // 2], ry.at[1 - a, (1 - b) // 2]
             else:
                 src, dst = pk, rx.at[(1 - a) // 2]
             return pltpu.make_async_remote_copy(
@@ -299,11 +307,13 @@
                 device_id=at(gx + a, b, c), device_id_type=MESH,
             )
 
-        def start():
-            for a, b, c in sorted(box, key=lambda o: -sum(map(abs, o))):
-                @pl.when(inside(gx, a, nx) & yz_ok(b, c))
-                def _(a=a, b=b, c=c):
-                    copy(a, b, c).start()
+        def start(far=(1, 2, 3)):
+            for n in sorted(far, reverse=True):
+                for a, b, c in box:
+                    if abs(a) + abs(b) + abs(c) == n:
+                        @pl.when(inside(gx, a, nx) & yz_ok(b, c))
+                        def _(a=a, b=b, c=c):
+                            copy(a, b, c).start()
 
         def wait():
             for a, b, c in box:
@@ -317,34 +327,54 @@
 
         return start, wait
 
-    def pack_box(get, pk, zp, a):
-        planes = [get(x) for x in range(4)]
-        lo, hi = zero8, zero8
-        for i in range(2):
-            pk[a, i] = jnp.where(own1, planes[2 * i], roll(planes[2 * i + 1], 64))
-        for x in range(4):
-            for t in range(4):
-                v = planes[x][8 * t : 8 * t + 8]
-                k = x * 4 + t
-                here = lane8 // 8 == k
-                lo = jnp.where(here, roll(v, (8 * k + 96) % 128), lo)
-                hi = jnp.where(here, roll(v, (8 * k + 40) % 128), hi)
-        zp[0, a] = lo
-        zp[1, a] = hi
-
-    def unpack_box(own, rx, ry, rz, a, put):
+    row8 = lax.broadcasted_iota(jnp.int32, (8, 128), 0)
+
+    def half(v):
+        return pltpu.roll(v, 4, 0)
+
+    def pack_box(gets, pk, xy, zp, yz):
+        edge = {(b, c): zero8 for b in range(2) for c in range(2)}
+        for a, get in enumerate(gets):
+            planes = [get(x) for x in range(4)]
+            pairs = [jnp.where(own1, planes[2 * i], roll(planes[2 * i + 1], 64)) for i in range(2)]
+            for i in range(2):
+                pk[a, i] = pairs[i]
+            xy[0, a] = jnp.where(row8 < 4, pairs[0][0:8], half(pairs[1][0:8]))
+            xy[1, a] = jnp.where(row8 >= 4, pairs[0][24:32], half(pairs[1][24:32]))
+            face = [zero8, zero8]
+            for x in range(4):
+                for t in range(4):
+                    v = planes[x][8 * t : 8 * t + 8]
+                    k = x * 4 + t
+                    for c, first in ((0, 96), (1, 40)):
+                        face[c] = jnp.where(lane8 // 8 == k, roll(v, (8 * k + first) % 128), face[c])
+                        if t in (0, 3):
+                            b = t // 3
+                            edge[b, c] = jnp.where(lane8 // 8 == 4 * a + x, roll(v, (32 * a + 8 * x + first) % 128), edge[b, c])
+            zp[0, a] = face[0]
+            zp[1, a] = face[1]
+        for b in range(2):
+            for c in range(2):
+                yz[b, c] = edge[b, c]
+
+    def unpack_box(own, rx, ry, rz, re, a, put):
+        def side(dx, x, c, first):
+            def corner(b):
+                return roll(re[dx, b, c], (first - 32 * a - 8 * x) % 128)
+
+            mid = [roll(rz[dx, c, a], (first - 8 * (4 * x + t)) % 128) for t in range(4)]
+            return jnp.concatenate([corner(0)] + mid + [corner(1)], axis=0)
+
         for dx in range(3):
             for x in range(4):
                 i = x // 2
                 turn = (lambda v: roll(v, 64)) if x % 2 else (lambda v: v)
+                flip = half if i else (lambda v: v)
                 mid = own(x) if dx == 1 else turn(rx[dx // 2, a, i])
-                centre = jnp.concatenate([turn(ry[dx, 0, a, i]), mid, turn(ry[dx, 1, a, i])], axis=0)
-                tiles = [(0, 3), (1, 0), (1, 1), (1, 2), (1, 3), (2, 0)]
-                left = jnp.concatenate([roll(rz[dx, dy, 0, a], (24 - 8 * (4 * x + t)) % 128) for dy, t in tiles], axis=0)
-                right = jnp.concatenate([roll(rz[dx, dy, 1, a], (96 - 8 * (4 * x + t)) % 128) for dy, t in tiles], axis=0)
-                out = jnp.where((lane48 >= 96) & (lane48 < 104), right, 0.0)
+                centre = jnp.concatenate([turn(flip(ry[dx, 0, a])), mid, turn(flip(ry[dx, 1, a]))], axis=0)
+                out = jnp.where((lane48 >= 96) & (lane48 < 104), side(dx, x, 1, 96), 0.0)
                 out = jnp.where((lane48 >= 32) & (lane48 < 96), centre, out)
-                out = jnp.where((lane48 >= 24) & (lane48 < 32), left, out)
+                out = jnp.where((lane48 >= 24) & (lane48 < 32), side(dx, x, 0, 24), out)
                 put(4 * dx + x, out)
 
     lane48 = lanes((48, 128))
@@ -380,10 +410,9 @@
 
     each(4, body)
     parts1 = (lambda x: d1[x], lambda x: fx1[x + 1], lambda x: fy1u[x], lambda x: fz1u[x])
-    for a, get in enumerate(parts1):
-        pack_box(get, pkc, zpc, a)
-    c_start, c_wait = box_exchange(pkc, zpc, rxc, ryc, rzc, s1c, r1c)
-    c_start()
+    pack_box(parts1, pkc, xyc, zpc, yzc)
+    c_start, c_wait = box_exchange(pkc, xyc, zpc, yzc, rxc, ryc, rzc, rec, s1c, r1c)
+    c_start((1, 2))
 
     def pack2(planes):
         out = zero8
@@ -462,15 +491,14 @@
         )
 
     cg = gather(cc, csx, crx, csn, crn)
-    cg[0]()
 
     wait()
     y_in(u0.at[0], yr0.at[0], 8, 64)
     sweep0(u0.at[0], u0.at[1], zr0.at[0], ys0.at[1], zs0.at[1], False)
     start, wait = round0(1)
     start()
-    cg[1]()
-    cg[2]()
+    c_start((3,))
+    cg[0]()
     wait()
     y_in(u0.at[1], yr0.at[1], 8, 64)
 
@@ -488,11 +516,11 @@
 
     each(4, body)
 
-    pack_box(lambda x: f1[x], pkf, zpf, 0)
-    f_start, f_wait = box_exchange(pkf, zpf, rxf, ryf, rzf, s1f, r1f)
+    pack_box([lambda x: f1[x]], pkf, xyf, zpf, yzf)
+    f_start, f_wait = box_exchange(pkf, xyf, zpf, yzf, rxf, ryf, rzf, ref_, s1f, r1f)
     f_start()
-    cg[3]()
-    cg[4]()
+    cg[1]()
+    cg[2]()
     c_wait()
     for a, get in enumerate(parts1):
         def put(p, out, a=a):
@@ -501,7 +529,7 @@
                 ok = out > 0.0
                 w1[p] = jnp.where(ok, W / jnp.where(ok, out, 1.0), 0.0)
 
-        unpack_box(get, rxc, ryc, rzc, a, put)
+        unpack_box(get, rxc, ryc, rzc, rec, a, put)
 
     def zero_rows(ref, n, rows):
         def body(p):
@@ -514,12 +542,14 @@
     for b in range(2):
         zero_rows(u1.at[b], 12, 48)
     f_wait()
+    cg[3]()
+    cg[4]()
 
     def put(p, out):
         f1e[p] = out
         u1[0, p, 8:56, :] = w1[p] * out
 
-    unpack_box(lambda x: f1[x], rxf, ryf, rzf, 0, put)
+    unpack_box(lambda x: f1[x], rxf, ryf, rzf, ref_, 0, put)
 
     def beside1(buf, p, r0, n):
         c = buf[p, r0 : r0 + n, :]
@@ -801,8 +831,10 @@
         V(3, 2, 8, 128), V(3, 2, 8, 128), V(3, 2, 8, 128), V(3, 2, 8, 128),
         V(2, 12, 64, 128), V(4, 32, 128), V(5, 32, 128), V(4, 32, 128), V(4, 32, 128), V(4, 32, 128), V(4, 32, 128),
         V(4, 32, 128), V(12, 48, 128), V(4, 12, 64, 128),
-        V(4, 2, 32, 128), V(2, 4, 8, 128), V(2, 4, 2, 32, 128), V(3, 2, 4, 2, 8, 128), V(3, 3, 2, 4, 8, 128),
-        V(1, 2, 32, 128), V(2, 1, 8, 128), V(2, 1, 2, 32, 128), V(3, 2, 1, 2, 8, 128), V(3, 3, 2, 1, 8, 128),
+        V(4, 2, 32, 128), V(2, 4, 8, 128), V(2, 4, 8, 128), V(2, 2, 8, 128),
+        V(2, 4, 2, 32, 128), V(3, 2, 4, 8, 128), V(3, 2, 4, 8, 128), V(3, 2, 2, 8, 128),
+        V(1, 2, 32, 128), V(2, 1, 8, 128), V(2, 1, 8, 128), V(2, 2, 8, 128),
+        V(2, 1, 2, 32, 128), V(3, 2, 1, 8, 128), V(3, 2, 1, 8, 128), V(3, 2, 2, 8, 128),
         M, M, M, M, V(256, 128), V(4, 2, 64, 128), V(6, 48, 128), V(6, 80, 128), V(6, 80, 128), V(4, 4, 48, 128),
         V(12, 48, 128),
         V(3, 3, 4, 4, 8, 128), V(3, 3, 4, 8, 128),

time: 46.7 us -> 43.7 us (0.936)
  Pallas kernels: 43.6 us -> 40.5 us
    pallas_call x1, Pallas kernels: 43.6 us -> 40.5 us  [on_device(): pl.pallas_call(kernel, out_shape=(shape, shape), in_specs=[pl.BlockSpec(m...]
where the time goes in v3:
time: 43.7 us; the launch traced here: 43.5 us
  Pallas kernels  40.5 us (93%)
  local copies, waits for them, and re-layouts  2.42 us (6%)
  between operations  0.65 us (1%)
    pallas_call x1, Pallas kernels, on_device(): pl.pallas_call(kernel, out_shape=(shape, shape), in_specs=[pl.BlockSpec(m...  40.5 us
    unnamed x4, local copies, waits for them, and re-layouts  2.42 us

profile of v3, /device:TPU:97, one launch (start us, length us, event | category | flops | bytes accessed | tf_op | source)
XLA Modules:
  0.0 43.5 jit_solution(11733440302647046816)
XLA Ops:
  0.6 40.5 %vcycle.1 = (f32[1,8,64,128]{3,2,1,0:T(8,128)}, f32[1,8,64,128]{3,2,1,0:T(8,128)}) custom-call(s32[8,64,128]{2,1,0:T(8,128)} %ph_h.1, f32[8,64,128]{2,1,0:T(8,128)} %de_h.1, f32[1,8,64,128]{3,2,1,0:T(8,128)} %rh_h.1), custom_call_target="tpu_custom_call" | custom-call | tf_op jit(solution)/shard_map/vcycle/pallas_call | solution.py:848
  41.1 0.0 copy-start
  41.1 1.7 %copy.7 = f32[1,8,64,128]{3,2,1,0:T(8,128)} copy(f32[1,8,64,128]{3,2,1,0:T(8,128)} %get-tuple-element.4) | data formatting | bytes 524288
  42.8 0.0 copy-done
  42.8 0.7 %copy.8 = f32[1,8,64,128]{3,2,1,0:T(8,128)} copy(f32[1,8,64,128]{3,2,1,0:T(8,128)S(1)} %copy-done) | data formatting | bytes 524288
Async XLA Ops:
  41.1 1.7 %copy-start = (f32[1,8,64,128]{3,2,1,0:T(8,128)S(1)}, f32[1,8,64,128]{3,2,1,0:T(8,128)}, u32[]{:S(2)}) copy-start(f32[1,8,64,128]{3,2,1,0:T(8,128)} %get-tuple-element.5) | copy-start | bytes 786436

commit v4 on v3

--- a/solution.py
+++ b/solution.py
@@ -54,7 +54,7 @@
 
 
 def kernel(
-    ph_h, de_h, rh_h, os_h, or_h,
+    ph_h, de_h, rh_h, osol, ores,
     ph, de, f0, rp, u0, fx, fy, fzu, fzd, w0, d0,
     rys, ryr, rzs, rzr, ys0, yr0, zs0, zr0,
     u1, f1, fx1, fy1u, fy1d, fz1u, fz1d, d1, w1, ce1,
@@ -63,8 +63,7 @@
     cc, gg,
     f2, u2, fx2, fy2, fz2, w2, d2,
     f3, u3, fx3, fy3, fz3, w3,
-    osol, ores,
-    in_sem, out_sem, rss, rrs, s0s, r0s, s1c, r1c, s1f, r1f, csx, crx, csn, crn, gs, gr,
+    in_sem, rss, rrs, s0s, r0s, s1c, r1c, s1f, r1f, csx, crx, csn, crn, gs, gr,
 ):
     gx, gy, gz = lax.axis_index("gx"), lax.axis_index("gy"), lax.axis_index("gz")
     nx, ny, nz = lax.axis_size("gx"), lax.axis_size("gy"), lax.axis_size("gz")
@@ -216,7 +215,7 @@
             new = c * THIRD + w0[x] * (f0[x] + s)
             keep0(dst, ys, x, new)
             if out:
-                osol[x] = d0[x] * new
+                osol[0, x] = d0[x] * new
             return pack0(carry, new, x)
 
         packed = loop(8, body, (zero8, zero8))
@@ -412,7 +411,7 @@
     parts1 = (lambda x: d1[x], lambda x: fx1[x + 1], lambda x: fy1u[x], lambda x: fz1u[x])
     pack_box(parts1, pkc, xyc, zpc, yzc)
     c_start, c_wait = box_exchange(pkc, xyc, zpc, yzc, rxc, ryc, rzc, rec, s1c, r1c)
-    c_start((1, 2))
+    c_start((1,2))
 
     def pack2(planes):
         out = zero8
@@ -493,15 +492,17 @@
     cg = gather(cc, csx, crx, csn, crn)
 
     wait()
+    c_start((3,))
+    cg[0]()
     y_in(u0.at[0], yr0.at[0], 8, 64)
     sweep0(u0.at[0], u0.at[1], zr0.at[0], ys0.at[1], zs0.at[1], False)
     start, wait = round0(1)
     start()
-    c_start((3,))
-    cg[0]()
     wait()
     y_in(u0.at[1], yr0.at[1], 8, 64)
 
+    cg[1]()
+    cg[2]()
     lo, hi = zr0[1, 0], zr0[1, 1]
 
     def body(i):
@@ -519,9 +520,9 @@
     pack_box([lambda x: f1[x]], pkf, xyf, zpf, yzf)
     f_start, f_wait = box_exchange(pkf, xyf, zpf, yzf, rxf, ryf, rzf, ref_, s1f, r1f)
     f_start()
-    cg[1]()
-    cg[2]()
     c_wait()
+    cg[3]()
+    cg[4]()
     for a, get in enumerate(parts1):
         def put(p, out, a=a):
             ce1[a, p, 8:56, :] = out
@@ -542,8 +543,6 @@
     for b in range(2):
         zero_rows(u1.at[b], 12, 48)
     f_wait()
-    cg[3]()
-    cg[4]()
 
     def put(p, out):
         f1e[p] = out
@@ -803,21 +802,15 @@
 
     start, wait = round0(0)
     start()
-    out0 = pltpu.make_async_copy(osol, os_h.at[0], out_sem.at[0])
-    out0.start()
     wait()
     y_in(u0.at[0], yr0.at[0], 8, 64)
     lo, hi = zr0[0, 0], zr0[0, 1]
 
     def body(x):
         c, s = beside0(u0.at[0], x, lo, hi)
-        ores[x] = f0[x] - d0[x] * c + s
+        ores[0, x] = f0[x] - d0[x] * c + s
 
     each(8, body)
-    out1 = pltpu.make_async_copy(ores, or_h.at[0], out_sem.at[1])
-    out1.start()
-    out0.wait()
-    out1.wait()
 
 
 def on_device(phase, density, rhs):
@@ -840,16 +833,15 @@
         V(3, 3, 4, 4, 8, 128), V(3, 3, 4, 8, 128),
         V(8, 48, 128), V(2, 12, 64, 128), V(9, 48, 128), V(8, 64, 128), V(8, 48, 128), V(8, 48, 128), V(8, 48, 128),
         V(4, 24, 128), V(2, 6, 40, 128), V(5, 24, 128), V(4, 40, 128), V(4, 24, 128), V(4, 24, 128),
-        V(8, 64, 128), V(8, 64, 128),
-        D(3), D(2), D(6), D(6), D(3, 6), D(3, 6), D(3, 3, 3), D(3, 3, 3), D(3, 3, 3), D(3, 3, 3),
+        D(3), D(6), D(6), D(3, 6), D(3, 6), D(3, 3, 3), D(3, 3, 3), D(3, 3, 3), D(3, 3, 3),
         D(3), D(3), D(4), D(4), D(4, 3, 3), D(4, 3, 3),
     ]
-    shape = jax.ShapeDtypeStruct(rhs.shape, F32)
+    near = pl.BlockSpec(memory_space=pltpu.VMEM)
     return pl.pallas_call(
         kernel,
-        out_shape=(shape, shape),
+        out_shape=(pltpu.VMEM(rhs.shape, F32),) * 2,
         in_specs=[pl.BlockSpec(memory_space=pl.ANY)] * 3,
-        out_specs=(pl.BlockSpec(memory_space=pl.ANY),) * 2,
+        out_specs=(near,) * 2,
         scratch_shapes=scratch,
         compiler_params=pltpu.CompilerParams(collective_id=0, has_side_effects=True),
         name="vcycle",

time: 43.7 us -> 41.4 us (0.947)
  Pallas kernels: 40.5 us -> 39.2 us
  local copies, waits for them, and re-layouts: 2.42 us -> 1.41 us
    pallas_call x1, Pallas kernels: 40.5 us -> 39.2 us  [on_device(): pl.pallas_call(kernel, out_shape=(pltpu.VMEM(rhs.shape, F32),) * 2, in_sp...]
    unnamed x4 -> x2, local copies, waits for them, and re-layouts: 2.42 us -> 1.41 us
where the time goes in v4:
time: 41.4 us; the launch traced here: 41.3 us
  Pallas kernels  39.2 us (95%)
  local copies, waits for them, and re-layouts  1.41 us (3%)
  between operations  0.64 us (2%)
    pallas_call x1, Pallas kernels, on_device(): pl.pallas_call(kernel, out_shape=(pltpu.VMEM(rhs.shape, F32),) * 2, in_sp...  39.2 us
    unnamed x2, local copies, waits for them, and re-layouts  1.41 us

profile of v4, /device:TPU:97, one launch (start us, length us, event | category | flops | bytes accessed | tf_op | source)
XLA Modules:
  0.0 41.3 jit_solution(16685286695742918998)
XLA Ops:
  0.6 39.2 %vcycle.1 = (f32[1,8,64,128]{3,2,1,0:T(8,128)S(1)}, f32[1,8,64,128]{3,2,1,0:T(8,128)S(1)}) custom-call(s32[8,64,128]{2,1,0:T(8,128)} %ph_h.1, f32[8,64,128]{2,1,0:T(8,128)} %de_h.1, f32[1,8,64,128]{3,2,1,0:T(8,128)} %rh_h.1), custom_call_target="tpu_custom_call" | custom-call | tf_op jit(solution)/shard_map/vcycle/pallas_call | solution.py:840
  39.9 0.7 %copy.7 = f32[1,8,64,128]{3,2,1,0:T(8,128)} copy(f32[1,8,64,128]{3,2,1,0:T(8,128)S(1)} %get-tuple-element.2) | data formatting | bytes 524288
  40.6 0.7 %copy.8 = f32[1,8,64,128]{3,2,1,0:T(8,128)} copy(f32[1,8,64,128]{3,2,1,0:T(8,128)S(1)} %get-tuple-element.3) | data formatting | bytes 524288

commit v5 on v4

--- a/solution.py
+++ b/solution.py
@@ -58,9 +58,9 @@
     ph, de, f0, rp, u0, fx, fy, fzu, fzd, w0, d0,
     rys, ryr, rzs, rzr, ys0, yr0, zs0, zr0,
     u1, f1, fx1, fy1u, fy1d, fz1u, fz1d, d1, w1, ce1,
-    pkc, xyc, zpc, yzc, rxc, ryc, rzc, rec, pkf, xyf, zpf, yzf, rxf, ryf, rzf, ref_,
+    pkc, xyc, zpc, xzc, yzc, rxc, ryc, rzc, rec, pkf, xyf, zpf, xzf, yzf, rxf, ryf, rzf, ref_,
     mb, mo, me, mt, t0, t1, t2, t3, t4, t5, f1e,
-    cc, gg,
+    cc, pz, zc, gg,
     f2, u2, fx2, fy2, fz2, w2, d2,
     f3, u3, fx3, fy3, fz3, w3,
     in_sem, rss, rrs, s0s, r0s, s1c, r1c, s1f, r1f, csx, crx, csn, crn, gs, gr,
@@ -109,12 +109,10 @@
 
     @pl.when(edge)
     def _():
-        for ref in (gg, rxc, rxf, ryf, rzf, ref_):
+        for ref in (gg, zc, rxc, rxf, ryf, rzf, ref_):
             ref[...] = jnp.zeros(ref.shape, F32)
-        for z in range(3):
-            for y in range(3):
-                if (z, y) != (1, 1):
-                    cc[z, y] = jnp.zeros(cc.shape[2:], F32)
+        for y in (0, 2):
+            cc[y] = jnp.zeros(cc.shape[1:], F32)
 
     def inside(at, step, count):
         return (at >= 0) if step == 0 else (at < count - 1) if step > 0 else (at > 0)
@@ -291,10 +289,12 @@
 
     box = [(a, b, c) for a in steps for b in steps for c in steps if (a, b, c) != (0, 0, 0)]
 
-    def box_exchange(pk, xy, zp, yz, rx, ry, rz, re, ss, rs):
+    def box_exchange(pk, xy, zp, xz, yz, rx, ry, rz, re, ss, rs):
         def copy(a, b, c):
             if b and c:
                 src, dst = yz.at[(b + 1) // 2, (c + 1) // 2], re.at[1 - a, (1 - b) // 2, (1 - c) // 2]
+            elif a and c:
+                src, dst = xz.at[(c + 1) // 2], rz.at[1 - a, (1 - c) // 2, pl.ds(0, xz.shape[1])]
             elif c:
                 src, dst = zp.at[(c + 1) // 2], rz.at[1 - a, (1 - c) // 2]
             elif b:
@@ -328,10 +328,12 @@
 
     row8 = lax.broadcasted_iota(jnp.int32, (8, 128), 0)
 
+    low4 = lane8 % 8 < 4
+
     def half(v):
         return pltpu.roll(v, 4, 0)
 
-    def pack_box(gets, pk, xy, zp, yz):
+    def pack_box(gets, pk, xy, zp, xz, yz):
         edge = {(b, c): zero8 for b in range(2) for c in range(2)}
         for a, get in enumerate(gets):
             planes = [get(x) for x in range(4)]
@@ -352,6 +354,14 @@
                             edge[b, c] = jnp.where(lane8 // 8 == 4 * a + x, roll(v, (32 * a + 8 * x + first) % 128), edge[b, c])
             zp[0, a] = face[0]
             zp[1, a] = face[1]
+            if a % 2 == 0:
+                even = face
+            if a % 2 == 1:
+                xz[0, a // 2] = jnp.where(low4, even[0], roll(face[0], 4))
+                xz[1, a // 2] = jnp.where(low4, roll(face[1], 124), even[1])
+            elif a == len(gets) - 1:
+                xz[0, a // 2] = face[0]
+                xz[1, a // 2] = face[1]
         for b in range(2):
             for c in range(2):
                 yz[b, c] = edge[b, c]
@@ -361,7 +371,8 @@
             def corner(b):
                 return roll(re[dx, b, c], (first - 32 * a - 8 * x) % 128)
 
-            mid = [roll(rz[dx, c, a], (first - 8 * (4 * x + t)) % 128) for t in range(4)]
+            shift, i = (0, a) if dx == 1 else ((4 - 8 * c) * (a % 2), a // 2)
+            mid = [roll(rz[dx, c, i], (first + shift - 8 * (4 * x + t)) % 128) for t in range(4)]
             return jnp.concatenate([corner(0)] + mid + [corner(1)], axis=0)
 
         for dx in range(3):
@@ -371,9 +382,9 @@
                 flip = half if i else (lambda v: v)
                 mid = own(x) if dx == 1 else turn(rx[dx // 2, a, i])
                 centre = jnp.concatenate([turn(flip(ry[dx, 0, a])), mid, turn(flip(ry[dx, 1, a]))], axis=0)
-                out = jnp.where((lane48 >= 96) & (lane48 < 104), side(dx, x, 1, 96), 0.0)
+                out = jnp.where((lane48 >= 96) & (lane48 < 100), side(dx, x, 1, 96), 0.0)
                 out = jnp.where((lane48 >= 32) & (lane48 < 96), centre, out)
-                out = jnp.where((lane48 >= 24) & (lane48 < 32), side(dx, x, 0, 24), out)
+                out = jnp.where((lane48 >= 28) & (lane48 < 32), side(dx, x, 0, 24), out)
                 put(4 * dx + x, out)
 
     lane48 = lanes((48, 128))
@@ -409,8 +420,8 @@
 
     each(4, body)
     parts1 = (lambda x: d1[x], lambda x: fx1[x + 1], lambda x: fy1u[x], lambda x: fz1u[x])
-    pack_box(parts1, pkc, xyc, zpc, yzc)
-    c_start, c_wait = box_exchange(pkc, xyc, zpc, yzc, rxc, ryc, rzc, rec, s1c, r1c)
+    pack_box(parts1, pkc, xyc, zpc, xzc, yzc)
+    c_start, c_wait = box_exchange(pkc, xyc, zpc, xzc, yzc, rxc, ryc, rzc, rec, s1c, r1c)
     c_start((1,2))
 
     def pack2(planes):
@@ -438,18 +449,18 @@
         zu.append(zu_)
         dg.append(xu_ + xd_ + yu_ + yd_ + zu_ + zd_)
     for a, planes in enumerate((dg, xu, yu, zu)):
-        cc[1, 1, gx, a] = pack2(planes)
-
-    def gather(buf, sx, rx, sn, rn):
+        cc[1, gx, a] = pack2(planes)
+
+    def gather(sx, rx, sn, rn):
         def xcopy(d):
             return pltpu.make_async_remote_copy(
-                src_ref=buf.at[1, 1, gx], dst_ref=buf.at[1, 1, gx], send_sem=sx.at[d - 1], recv_sem=rx.at[d - 1],
+                src_ref=cc.at[1, gx], dst_ref=cc.at[1, gx], send_sem=sx.at[d - 1], recv_sem=rx.at[d - 1],
                 device_id={"gx": lax.rem(gx + d, nx)}, device_id_type=MESH,
             )
 
         def ncopy(d):
-            src = buf.at[1, 1] if d < 4 else buf.at[1]
-            dst = [buf.at[1, 0], buf.at[1, 2], buf.at[0], buf.at[2]][d - 2]
+            src = [cc.at[1], cc.at[1], pz.at[1], pz.at[0]][d - 2]
+            dst = [cc.at[0], cc.at[2], zc.at[0], zc.at[1]][d - 2]
             return pltpu.make_async_remote_copy(
                 src_ref=src, dst_ref=dst, send_sem=sn.at[d - 2], recv_sem=rn.at[d - 2],
                 device_id=near[d][0], device_id_type=MESH,
@@ -462,7 +473,7 @@
         def xwait():
             for d in range(1, 4):
                 pltpu.make_async_remote_copy(
-                    src_ref=buf.at[1, 1, gx], dst_ref=buf.at[1, 1, lax.rem(gx + 4 - d, nx)],
+                    src_ref=cc.at[1, gx], dst_ref=cc.at[1, lax.rem(gx + 4 - d, nx)],
                     send_sem=sx.at[d - 1], recv_sem=rx.at[d - 1],
                     device_id={"gx": lax.rem(gx + d, nx)}, device_id_type=MESH,
                 ).wait()
@@ -489,7 +500,7 @@
             lambda: nstart((4, 5)), lambda: nwait((4, 5)),
         )
 
-    cg = gather(cc, csx, crx, csn, crn)
+    cg = gather(csx, crx, csn, crn)
 
     wait()
     c_start((3,))
@@ -517,11 +528,21 @@
 
     each(4, body)
 
-    pack_box([lambda x: f1[x]], pkf, xyf, zpf, yzf)
-    f_start, f_wait = box_exchange(pkf, xyf, zpf, yzf, rxf, ryf, rzf, ref_, s1f, r1f)
+    pack_box([lambda x: f1[x]], pkf, xyf, zpf, xzf, yzf)
+    f_start, f_wait = box_exchange(pkf, xyf, zpf, xzf, yzf, rxf, ryf, rzf, ref_, s1f, r1f)
     f_start()
     c_wait()
     cg[3]()
+    low16 = lane8 % 32 < 16
+
+    def body(y):
+        for b in range(4):
+            for j in range(2):
+                v, w = cc[y, b, 2 * j], cc[y, b, 2 * j + 1]
+                pz[0, y, b, j] = jnp.where(low16, v, roll(w, 16))
+                pz[1, y, b, j] = jnp.where(low16, roll(w, 112), v)
+
+    each(3, body)
     cg[4]()
     for a, get in enumerate(parts1):
         def put(p, out, a=a):
@@ -622,18 +643,18 @@
     g_start()
     cg[5]()
 
-    def spread2(get, put):
+    def spread2(get, put, shift, reach):
         def body(b):
             for y in range(3):
                 v = [get(z, y, b) for z in range(3)]
                 for x in range(2):
                     for t in range(2):
                         g = 2 * x + t
-                        left = roll(v[0], (16 - 32 * g) % 128)
+                        left = roll(v[0], (16 - 32 * g + shift) % 128)
                         mid = roll(v[1], (48 - 32 * g) % 128)
-                        right = roll(v[2], (80 - 32 * g) % 128)
+                        right = roll(v[2], (80 - 32 * g - shift) % 128)
                         out = jnp.where(lane8 < 48, left, jnp.where(lane8 < 80, mid, right))
-                        out = jnp.where((lane8 >= 16) & (lane8 < 112), out, 0.0)
+                        out = jnp.where((lane8 >= 48 - reach) & (lane8 < 80 + reach), out, 0.0)
                         put(2 * b + x, 16 * y + 8 * t, out)
 
         each(4, body)
@@ -657,7 +678,7 @@
         u2[0, p + 2, 8 + r : 16 + r, :] = w2[p, r : r + 8, :] * v
 
     for a, put in enumerate((put_d, put_x, put_y, put_z)):
-        spread2(lambda z, y, b, a=a: cc[z, y, b, a], put)
+        spread2(lambda z, y, b, a=a: cc[y, b, a] if z == 1 else zc[z // 2, y, b, a // 2], put, 16 * (a % 2), 16)
     fx2[0] = jnp.zeros((48, 128), F32)
     fx3[0] = jnp.zeros((24, 128), F32)
 
@@ -694,7 +715,7 @@
     each(4, body)
 
     g_wait()
-    spread2(lambda z, y, b: gg[z, y, b], put_f)
+    spread2(lambda z, y, b: gg[z, y, b], put_f, 0, 32)
 
     def beside(buf, fxr, fyr, fzr, p, rows):
         c = buf[p + 1, 8 : 8 + rows, :]
@@ -811,6 +832,14 @@
         ores[0, x] = f0[x] - d0[x] * c + s
 
     each(8, body)
+
+
+def flush(a, b, oa, ob, sem):
+    copies = [pltpu.make_async_copy(a, oa, sem.at[0]), pltpu.make_async_copy(b, ob, sem.at[1])]
+    for c in copies:
+        c.start()
+    for c in copies:
+        c.wait()
 
 
 def on_device(phase, density, rhs):
@@ -824,20 +853,20 @@
         V(3, 2, 8, 128), V(3, 2, 8, 128), V(3, 2, 8, 128), V(3, 2, 8, 128),
         V(2, 12, 64, 128), V(4, 32, 128), V(5, 32, 128), V(4, 32, 128), V(4, 32, 128), V(4, 32, 128), V(4, 32, 128),
         V(4, 32, 128), V(12, 48, 128), V(4, 12, 64, 128),
-        V(4, 2, 32, 128), V(2, 4, 8, 128), V(2, 4, 8, 128), V(2, 2, 8, 128),
+        V(4, 2, 32, 128), V(2, 4, 8, 128), V(2, 4, 8, 128), V(2, 2, 8, 128), V(2, 2, 8, 128),
         V(2, 4, 2, 32, 128), V(3, 2, 4, 8, 128), V(3, 2, 4, 8, 128), V(3, 2, 2, 8, 128),
-        V(1, 2, 32, 128), V(2, 1, 8, 128), V(2, 1, 8, 128), V(2, 2, 8, 128),
+        V(1, 2, 32, 128), V(2, 1, 8, 128), V(2, 1, 8, 128), V(2, 1, 8, 128), V(2, 2, 8, 128),
         V(2, 1, 2, 32, 128), V(3, 2, 1, 8, 128), V(3, 2, 1, 8, 128), V(3, 2, 2, 8, 128),
         M, M, M, M, V(256, 128), V(4, 2, 64, 128), V(6, 48, 128), V(6, 80, 128), V(6, 80, 128), V(4, 4, 48, 128),
         V(12, 48, 128),
-        V(3, 3, 4, 4, 8, 128), V(3, 3, 4, 8, 128),
+        V(3, 4, 4, 8, 128), V(2, 3, 4, 2, 8, 128), V(2, 3, 4, 2, 8, 128), V(3, 3, 4, 8, 128),
         V(8, 48, 128), V(2, 12, 64, 128), V(9, 48, 128), V(8, 64, 128), V(8, 48, 128), V(8, 48, 128), V(8, 48, 128),
         V(4, 24, 128), V(2, 6, 40, 128), V(5, 24, 128), V(4, 40, 128), V(4, 24, 128), V(4, 24, 128),
         D(3), D(6), D(6), D(3, 6), D(3, 6), D(3, 3, 3), D(3, 3, 3), D(3, 3, 3), D(3, 3, 3),
         D(3), D(3), D(4), D(4), D(4, 3, 3), D(4, 3, 3),
     ]
     near = pl.BlockSpec(memory_space=pltpu.VMEM)
-    return pl.pallas_call(
+    pair = pl.pallas_call(
         kernel,
         out_shape=(pltpu.VMEM(rhs.shape, F32),) * 2,
         in_specs=[pl.BlockSpec(memory_space=pl.ANY)] * 3,
@@ -846,6 +875,15 @@
         compiler_params=pltpu.CompilerParams(collective_id=0, has_side_effects=True),
         name="vcycle",
     )(phase, density, rhs)
+    pair = [pltpu.with_memory_space_constraint(v, pltpu.VMEM) for v in pair]
+    return pl.pallas_call(
+        flush,
+        out_shape=(jax.ShapeDtypeStruct(rhs.shape, F32),) * 2,
+        in_specs=[near] * 2,
+        out_specs=(pl.BlockSpec(memory_space=pl.ANY),) * 2,
+        scratch_shapes=[D(2)],
+        name="flush",
+    )(*pair)
 
 
 def solution(mesh):

time: 41.4 us -> 39.9 us (0.964)
  local copies, waits for them, and re-layouts: 1.41 us -> 0 us
    unnamed x2 -> x0, local copies, waits for them, and re-layouts: 1.41 us -> none
    pallas_call x1, Pallas kernels: 39.2 us -> 38.3 us  [on_device(): pl.pallas_call(kernel, out_shape=(pltpu.VMEM(rhs.shape, F32),) * 2, in_sp...]
    pallas_call x0 -> x1, Pallas kernels: none -> 0.81 us  [on_device(): pl.pallas_call(flush, out_shape=(jax.ShapeDtypeStruct(rhs.shape, F32),) *...]
where the time goes in v5:
time: 39.9 us; the launch traced here: 39.8 us
  Pallas kernels  39.1 us (98%)
  between operations  0.64 us (2%)
    pallas_call x1, Pallas kernels, on_device(): pl.pallas_call(kernel, out_shape=(pltpu.VMEM(rhs.shape, F32),) * 2, in_sp...  38.3 us
    pallas_call x1, Pallas kernels, on_device(): pl.pallas_call(flush, out_shape=(jax.ShapeDtypeStruct(rhs.shape, F32),) *...  0.81 us

profile of v5, /device:TPU:97, one launch (start us, length us, event | category | flops | bytes accessed | tf_op | source)
XLA Modules:
  0.0 39.8 jit_solution(16254395382685036512)
XLA Ops:
  0.6 38.3 %vcycle.1 = (f32[1,8,64,128]{3,2,1,0:T(8,128)S(1)}, f32[1,8,64,128]{3,2,1,0:T(8,128)S(1)}) custom-call(s32[8,64,128]{2,1,0:T(8,128)} %ph_h.1, f32[8,64,128]{2,1,0:T(8,128)} %de_h.1, f32[1,8,64,128]{3,2,1,0:T(8,128)} %rh_h.1), custom_call_target="tpu_custom_call" | custom-call | tf_op jit(solution)/shard_map/vcycle/pallas_call | solution.py:869
  38.9 0.8 %flush.1 = (f32[1,8,64,128]{3,2,1,0:T(8,128)}, f32[1,8,64,128]{3,2,1,0:T(8,128)}) custom-call(f32[1,8,64,128]{3,2,1,0:T(8,128)S(1)} %get-tuple-element.4.a, f32[1,8,64,128]{3,2,1,0:T(8,128)S(1)} %get-tuple-element.5.b), custom_call_target="tpu_custom_call" | custom-call | tf_op jit(solution)/shard_map/flush/pallas_call | solution.py:879

commit v6 on v5

--- a/solution.py
+++ b/solution.py
@@ -55,7 +55,7 @@
 
 def kernel(
     ph_h, de_h, rh_h, osol, ores,
-    ph, de, f0, rp, u0, fx, fy, fzu, fzd, w0, d0,
+    ph, de, f0, part, fze, rp, u0, fx, fy, fzu, fzd, w0, d0,
     rys, ryr, rzs, rzr, ys0, yr0, zs0, zr0,
     u1, f1, fx1, fy1u, fy1d, fz1u, fz1d, d1, w1, ce1,
     pkc, xyc, zpc, xzc, yzc, rxc, ryc, rzc, rec, pkf, xyf, zpf, xzf, yzf, rxf, ryf, rzf, ref_,
@@ -197,28 +197,69 @@
 
         each(n, body)
 
-    def beside0(buf, x, lo, hi):
+    def mod(v):
+        return v % 128 if isinstance(v, int) else lax.rem(v, 128)
+
+    def packz(acc, plane, x):
+        for t in range(8):
+            v = plane[8 * t : 8 * t + 8]
+            k = 2 * (x * 8 + t)
+            acc = jnp.where(lane8 == k, roll(v, mod(k + 1)), acc)
+            acc = jnp.where(lane8 == mod(k + 127), roll(v, mod(k + 127)), acc)
+        return acc
+
+    def heldz(zr):
+        return jnp.where(lane8 % 2 == 0, zr[0], zr[1])
+
+    def keepu(buf, ys, x, plane):
+        keep0(buf, ys, x, plane)
+        buf[x + 1, 7:8, :] = jnp.zeros((1, 128), F32)
+        buf[x + 1, 72:73, :] = jnp.zeros((1, 128), F32)
+
+    def within0(buf, x, whole):
         c = buf[x + 1, 8:72, :]
-        up, down = z_beside0(c, x, lo, hi)
-        s = fx[x + 1] * buf[x + 2, 8:72, :] + fx[x] * buf[x, 8:72, :]
-        s = s + fy[x, 8:72, :] * buf[x + 1, 9:73, :] + fy[x, 7:71, :] * buf[x + 1, 7:71, :]
-        s = s + fzu[x] * up + fzd[x] * down
+        s = fy[x, 8:72, :] * buf[x + 1, 9:73, :] + fy[x, 7:71, :] * buf[x + 1, 7:71, :]
+        s = s + fzu[x] * jnp.where(lane64 == 127, 0.0, roll(c, 127))
+        s = s + fzd[x] * jnp.where(lane64 == 0, 0.0, roll(c, 1))
+        if whole or x < 7:
+            s = s + fx[x + 1] * buf[x + 2, 8:72, :]
+        if whole or x > 0:
+            s = s + fx[x] * buf[x, 8:72, :]
         return c, s
 
-    def sweep0(src, dst, zr, ys, zs, out):
-        lo, hi = zr[0], zr[1]
-
-        def body(x, carry):
-            c, s = beside0(src, x, lo, hi)
-            new = c * THIRD + w0[x] * (f0[x] + s)
-            keep0(dst, ys, x, new)
+    def zface0(x, held):
+        return fze[x] * jnp.concatenate([roll(held, mod(256 - 2 * (x * 8 + t))) for t in range(8)], axis=0)
+
+    def across0(buf, yr, held, x):
+        h = zface0(x, held)
+        if x == 0:
+            h = h + fx[0] * buf[0, 8:72, :]
+        if x == 7:
+            h = h + fx[8] * buf[9, 8:72, :]
+        top = fy[x, 7:8, :] * yr[0, x : x + 1, :]
+        end = fy[x, 71:72, :] * yr[1, x : x + 1, :]
+        return jnp.concatenate(
+            [h[0:8] + jnp.where(row8 == 0, top, 0.0), h[8:56], h[56:64] + jnp.where(row8 == 7, end, 0.0)], axis=0
+        )
+
+    def inner0(buf, resid):
+        for x in range(8):
+            c, s = within0(buf, x, False)
+            part[x] = f0[x] - d0[x] * c + s if resid else c * THIRD + w0[x] * (f0[x] + s)
+
+    def outer0(src, yr, zr, dst, ys, zs, out):
+        held = heldz(zr)
+        acc = zero8
+        for x in range(8):
+            new = part[x] + w0[x] * across0(src, yr, held, x)
+            keepu(dst, ys, x, new)
             if out:
                 osol[0, x] = d0[x] * new
-            return pack0(carry, new, x)
-
-        packed = loop(8, body, (zero8, zero8))
-        zs[0] = packed[0]
-        zs[1] = packed[1]
+            acc = packz(acc, new, x)
+        zs[0] = acc
+        zs[1] = acc
+
+    row8 = lax.broadcasted_iota(jnp.int32, (8, 128), 0)
 
     for c in loads[:2]:
         c.wait()
@@ -277,12 +318,13 @@
         w = W / diag
         w0[x] = w
         first = w * f0[x]
-        keep0(u0.at[0], ys0.at[0], x, first)
-        return pack0(carry, first, x)
-
-    packed = loop(8, body, (zero8, zero8))
-    zs0[0, 0] = packed[0]
-    zs0[0, 1] = packed[1]
+        fze[x] = jnp.where(lane64 == 127, zu, jnp.where(lane64 == 0, zd, 0.0))
+        keepu(u0.at[0], ys0.at[0], x, first)
+        return packz(carry, first, x)
+
+    packed = loop(8, body, zero8)
+    zs0[0, 0] = packed
+    zs0[0, 1] = packed
 
     def round0(b):
         return faces(u0.at[b], 8, 64, ys0.at[b], yr0.at[b], zs0.at[b], zr0.at[b], s0s.at[b], r0s.at[b])
@@ -325,8 +367,6 @@
                     copy(a, b, c).wait_recv()
 
         return start, wait
-
-    row8 = lax.broadcasted_iota(jnp.int32, (8, 128), 0)
 
     low4 = lane8 % 8 < 4
 
@@ -502,31 +542,27 @@
 
     cg = gather(csx, crx, csn, crn)
 
+    inner0(u0.at[0], False)
     wait()
     c_start((3,))
     cg[0]()
-    y_in(u0.at[0], yr0.at[0], 8, 64)
-    sweep0(u0.at[0], u0.at[1], zr0.at[0], ys0.at[1], zs0.at[1], False)
+    outer0(u0.at[0], yr0.at[0], zr0.at[0], u0.at[1], ys0.at[1], zs0.at[1], False)
     start, wait = round0(1)
     start()
+    inner0(u0.at[1], True)
     wait()
-    y_in(u0.at[1], yr0.at[1], 8, 64)
 
     cg[1]()
     cg[2]()
-    lo, hi = zr0[1, 0], zr0[1, 1]
-
-    def body(i):
+    held = heldz(zr0.at[1])
+    for i in range(4):
         total = None
         for j in range(2):
             x = 2 * i + j
-            c, s = beside0(u0.at[1], x, lo, hi)
-            r = f0[x] - d0[x] * c + s
+            r = part[x] + across0(u0.at[1], yr0.at[1], held, x)
             total = r if total is None else total + r
         t1[i, 0] = total
         f1[i] = mm(t1[i, 0, pl.ds(0, 32, stride=2), :] + t1[i, 0, pl.ds(1, 32, stride=2), :], mb[...])
-
-    each(4, body)
 
     pack_box([lambda x: f1[x]], pkf, xyf, zpf, xzf, yzf)
     f_start, f_wait = box_exchange(pkf, xyf, zpf, xzf, yzf, rxf, ryf, rzf, ref_, s1f, r1f)
@@ -795,43 +831,44 @@
 
     each(6, body)
 
+    y_in(u0.at[1], yr0.at[1], 8, 64)
+
     def body(p):
         u0[0, p, :, :] = u0[1, p, :, :] + t3[(p + 1) // 2]
 
     each(10, body)
 
-    def body(q, carry):
-        lo, hi = carry
+    held = heldz(zr0.at[1])
+    extra = zero8
+    for q in range(4):
         for t in range(8):
             v = t4[q + 1, 8 + 8 * t : 16 + 8 * t, :]
-            k = 16 * q + t
-            here = (lane8 == k) | (lane8 == k + 8)
-            a, b = roll(v, lax.rem(k + 97, 128)), roll(v, lax.rem(k + 32, 128))
-            lo = jnp.where(lane8 == k, a, jnp.where(lane8 == k + 8, roll(a, 8), lo))
-            hi = jnp.where(lane8 == k, b, jnp.where(lane8 == k + 8, roll(b, 8), hi))
-        return lo, hi
-
-    lo, hi = loop(4, body, (zero8, zero8))
-    zr0[0, 0] = zr0[1, 0] + lo
-    zr0[0, 1] = zr0[1, 1] + hi
-    sweep0(u0.at[0], u0.at[2], zr0.at[0], ys0.at[2], zs0.at[2], False)
+            k = 2 * (16 * q + t)
+            up, down = roll(v, (k - 31) % 128), roll(v, (k - 97) % 128)
+            extra = jnp.where(lane8 == k, up, jnp.where(lane8 == (k + 127) % 128, down, extra))
+            extra = jnp.where(lane8 == k + 16, roll(up, 16), jnp.where(lane8 == k + 15, roll(down, 16), extra))
+    held = held + extra
+    acc = zero8
+    for x in range(8):
+        c, s = within0(u0.at[0], x, True)
+        new = c * THIRD + w0[x] * (f0[x] + s + zface0(x, held))
+        keepu(u0.at[2], ys0.at[2], x, new)
+        acc = packz(acc, new, x)
+    zs0[2, 0] = acc
+    zs0[2, 1] = acc
     start, wait = round0(2)
     start()
+    inner0(u0.at[2], False)
     wait()
-    y_in(u0.at[2], yr0.at[2], 8, 64)
-    sweep0(u0.at[2], u0.at[0], zr0.at[2], ys0.at[0], zs0.at[0], True)
-
-    start, wait = round0(0)
+    outer0(u0.at[2], yr0.at[2], zr0.at[2], u0.at[1], ys0.at[1], zs0.at[1], True)
+
+    start, wait = round0(1)
     start()
+    inner0(u0.at[1], True)
     wait()
-    y_in(u0.at[0], yr0.at[0], 8, 64)
-    lo, hi = zr0[0, 0], zr0[0, 1]
-
-    def body(x):
-        c, s = beside0(u0.at[0], x, lo, hi)
-        ores[0, x] = f0[x] - d0[x] * c + s
-
-    each(8, body)
+    held = heldz(zr0.at[1])
+    for x in range(8):
+        ores[0, x] = part[x] + across0(u0.at[1], yr0.at[1], held, x)
 
 
 def flush(a, b, oa, ob, sem):
@@ -847,7 +884,7 @@
     M = pltpu.VMEM((384, 128), BF16)
     D = lambda *s: pltpu.SemaphoreType.DMA(s)
     scratch = [
-        pltpu.VMEM((8, 64, 128), jnp.int32), V(8, 64, 128), V(8, 64, 128), V(10, 80, 128), V(3, 10, 80, 128),
+        pltpu.VMEM((8, 64, 128), jnp.int32), V(8, 64, 128), V(8, 64, 128), V(8, 64, 128), V(8, 64, 128), V(10, 80, 128), V(3, 10, 80, 128),
         V(9, 64, 128), V(8, 80, 128), V(8, 64, 128), V(8, 64, 128), V(8, 64, 128), V(8, 64, 128),
         V(2, 8, 128), V(2, 8, 128), V(2, 8, 128), V(2, 8, 128),
         V(3, 2, 8, 128), V(3, 2, 8, 128), V(3, 2, 8, 128), V(3, 2, 8, 128),

time: 39.9 us -> 39.5 us (0.990)
  no operation moved by 1% of the time
where the time goes in v6:
time: 39.5 us; the launch traced here: 39.4 us
  Pallas kernels  38.8 us (98%)
  between operations  0.64 us (2%)
    pallas_call x1, Pallas kernels, on_device(): pl.pallas_call(kernel, out_shape=(pltpu.VMEM(rhs.shape, F32),) * 2, in_sp...  38 us
    pallas_call x1, Pallas kernels, on_device(): pl.pallas_call(flush, out_shape=(jax.ShapeDtypeStruct(rhs.shape, F32),) *...  0.81 us

profile of v6, /device:TPU:97, one launch (start us, length us, event | category | flops | bytes accessed | tf_op | source)
XLA Modules:
  0.0 39.4 jit_solution(9180475631565929998)
XLA Ops:
  0.6 38.0 %vcycle.1 = (f32[1,8,64,128]{3,2,1,0:T(8,128)S(1)}, f32[1,8,64,128]{3,2,1,0:T(8,128)S(1)}) custom-call(s32[8,64,128]{2,1,0:T(8,128)} %ph_h.1, f32[8,64,128]{2,1,0:T(8,128)} %de_h.1, f32[1,8,64,128]{3,2,1,0:T(8,128)} %rh_h.1), custom_call_target="tpu_custom_call" | custom-call | tf_op jit(solution)/shard_map/vcycle/pallas_call | solution.py:906
  38.6 0.8 %flush.1 = (f32[1,8,64,128]{3,2,1,0:T(8,128)}, f32[1,8,64,128]{3,2,1,0:T(8,128)}) custom-call(f32[1,8,64,128]{3,2,1,0:T(8,128)S(1)} %get-tuple-element.4.a, f32[1,8,64,128]{3,2,1,0:T(8,128)S(1)} %get-tuple-element.5.b), custom_call_target="tpu_custom_call" | custom-call | tf_op jit(solution)/shard_map/flush/pallas_call | solution.py:916

commit v7 on v6

--- a/solution.py
+++ b/solution.py
@@ -100,16 +100,12 @@
         def _(where=where):
             pl.semaphore_signal(barrier, inc=1, device_id=where, device_id_type=MESH)
 
-    for b in range(3):
-        for x in (0, 9):
-            u0[b, x, 8:72, :] = jnp.zeros((64, 128), F32)
-        for ref in (yr0, zr0):
-            for k in range(2):
-                ref[b, k] = jnp.zeros((8, 128), F32)
-
     @pl.when(edge)
     def _():
-        for ref in (gg, zc, rxc, rxf, ryf, rzf, ref_):
+        for b in range(3):
+            for x in (0, 9):
+                u0[b, x, 8:72, :] = jnp.zeros((64, 128), F32)
+        for ref in (yr0, zr0, gg, zc, rxc, rxf, ryf, rzf, ref_):
             ref[...] = jnp.zeros(ref.shape, F32)
         for y in (0, 2):
             cc[y] = jnp.zeros(cc.shape[1:], F32)
@@ -567,7 +563,6 @@
     pack_box([lambda x: f1[x]], pkf, xyf, zpf, xzf, yzf)
     f_start, f_wait = box_exchange(pkf, xyf, zpf, xzf, yzf, rxf, ryf, rzf, ref_, s1f, r1f)
     f_start()
-    c_wait()
     cg[3]()
     low16 = lane8 % 32 < 16
 
@@ -580,6 +575,7 @@
 
     each(3, body)
     cg[4]()
+    c_wait()
     for a, get in enumerate(parts1):
         def put(p, out, a=a):
             ce1[a, p, 8:56, :] = out
@@ -753,18 +749,20 @@
     g_wait()
     spread2(lambda z, y, b: gg[z, y, b], put_f, 0, 32)
 
-    def beside(buf, fxr, fyr, fzr, p, rows):
-        c = buf[p + 1, 8 : 8 + rows, :]
-        s = fxr[p + 1] * buf[p + 2, 8 : 8 + rows, :] + fxr[p] * buf[p, 8 : 8 + rows, :]
-        s = s + fyr[p, 8 : 8 + rows, :] * buf[p + 1, 9 : 9 + rows, :]
-        s = s + fyr[p, 7 : 7 + rows, :] * buf[p + 1, 7 : 7 + rows, :]
-        z = fzr[p]
+    def beside(buf, fxr, fyr, fzr, p, rows, o=0):
+        a, b = o + 8, o + 8 + rows
+        c = buf[p + 1, a:b, :]
+        s = fxr[p + 1, o : o + rows, :] * buf[p + 2, a:b, :] + fxr[p, o : o + rows, :] * buf[p, a:b, :]
+        s = s + fyr[p, a:b, :] * buf[p + 1, a + 1 : b + 1, :]
+        s = s + fyr[p, a - 1 : b - 1, :] * buf[p + 1, a - 1 : b - 1, :]
+        z = fzr[p, o : o + rows, :]
         return c, s + z * roll(c, 127) + roll(z * c, 1)
 
-    def sweep2(src, dst):
+    def sweep2(src, dst, o, rows):
         def body(p):
-            c, s = beside(u2.at[src, pl.ds(1, 10)], fx2, fy2, fz2, p, 48)
-            u2[dst, p + 2, 8:56, :] = c * THIRD + w2[p] * (f2[p] + s)
+            c, s = beside(u2.at[src, pl.ds(1, 10)], fx2, fy2, fz2, p, rows, o)
+            here = slice(o, o + rows)
+            u2[dst, p + 2, o + 8 : o + 8 + rows, :] = c * THIRD + w2[p, here, :] * (f2[p, here, :] + s)
 
         each(8, body)
 
@@ -775,7 +773,7 @@
 
         each(4, body)
 
-    sweep2(0, 1)
+    sweep2(0, 1, 0, 48)
 
     def body(p):
         total = None
@@ -803,8 +801,8 @@
             u2[0, q + 2, 8:56, :] = u2[1, q + 2, 8:56, :] + jnp.where(d2[q] > 0.0, wide, 0.0)
 
     each(4, body)
-    sweep2(0, 1)
-    sweep2(1, 0)
+    sweep2(0, 1, 8, 32)
+    sweep2(1, 0, 8, 32)
 
     def body(q):
         e = mm(u2[0, 2 * gx + q, 20:44, :], mt[...])

time: 39.5 us -> 39.6 us (level)
  no operation moved by 1% of the time
where the time goes in v7:
time: 39.6 us; the launch traced here: 39.5 us
  Pallas kernels  38.8 us (98%)
  between operations  0.64 us (2%)
    pallas_call x1, Pallas kernels, on_device(): pl.pallas_call(kernel, out_shape=(pltpu.VMEM(rhs.shape, F32),) * 2, in_sp...  38 us
    pallas_call x1, Pallas kernels, on_device(): pl.pallas_call(flush, out_shape=(jax.ShapeDtypeStruct(rhs.shape, F32),) *...  0.81 us

profile of v7, /device:TPU:97, one launch (start us, length us, event | category | flops | bytes accessed | tf_op | source)
XLA Modules:
  0.0 39.5 jit_solution(14383717399098504811)
XLA Ops:
  0.6 38.0 %vcycle.1 = (f32[1,8,64,128]{3,2,1,0:T(8,128)S(1)}, f32[1,8,64,128]{3,2,1,0:T(8,128)S(1)}) custom-call(s32[8,64,128]{2,1,0:T(8,128)} %ph_h.1, f32[8,64,128]{2,1,0:T(8,128)} %de_h.1, f32[1,8,64,128]{3,2,1,0:T(8,128)} %rh_h.1), custom_call_target="tpu_custom_call" | custom-call | tf_op jit(solution)/shard_map/vcycle/pallas_call | solution.py:904
  38.7 0.8 %flush.1 = (f32[1,8,64,128]{3,2,1,0:T(8,128)}, f32[1,8,64,128]{3,2,1,0:T(8,128)}) custom-call(f32[1,8,64,128]{3,2,1,0:T(8,128)S(1)} %get-tuple-element.4.a, f32[1,8,64,128]{3,2,1,0:T(8,128)S(1)} %get-tuple-element.5.b), custom_call_target="tpu_custom_call" | custom-call | tf_op jit(solution)/shard_map/flush/pallas_call | solution.py:914

commit v8 on v7

--- a/solution.py
+++ b/solution.py
@@ -140,7 +140,7 @@
             )
 
         def start():
-            for d in range(6):
+            for d in (4, 5, 2, 3, 0, 1):
                 @pl.when(near[d][1])
                 def _(d=d):
                     copy(d).start()

time: 39.6 us -> 39.5 us (level)
  no operation moved by 1% of the time
where the time goes in v8:
time: 39.5 us; the launch traced here: 39.4 us
  Pallas kernels  38.8 us (98%)
  between operations  0.64 us (2%)
    pallas_call x1, Pallas kernels, on_device(): pl.pallas_call(kernel, out_shape=(pltpu.VMEM(rhs.shape, F32),) * 2, in_sp...  38 us
    pallas_call x1, Pallas kernels, on_device(): pl.pallas_call(flush, out_shape=(jax.ShapeDtypeStruct(rhs.shape, F32),) *...  0.81 us

profile of v8, /device:TPU:97, one launch (start us, length us, event | category | flops | bytes accessed | tf_op | source)
XLA Modules:
  0.0 39.4 jit_solution(7413436705030443511)
XLA Ops:
  0.6 38.0 %vcycle.1 = (f32[1,8,64,128]{3,2,1,0:T(8,128)S(1)}, f32[1,8,64,128]{3,2,1,0:T(8,128)S(1)}) custom-call(s32[8,64,128]{2,1,0:T(8,128)} %ph_h.1, f32[8,64,128]{2,1,0:T(8,128)} %de_h.1, f32[1,8,64,128]{3,2,1,0:T(8,128)} %rh_h.1), custom_call_target="tpu_custom_call" | custom-call | tf_op jit(solution)/shard_map/vcycle/pallas_call | solution.py:904
  38.6 0.8 %flush.1 = (f32[1,8,64,128]{3,2,1,0:T(8,128)}, f32[1,8,64,128]{3,2,1,0:T(8,128)}) custom-call(f32[1,8,64,128]{3,2,1,0:T(8,128)S(1)} %get-tuple-element.4.a, f32[1,8,64,128]{3,2,1,0:T(8,128)S(1)} %get-tuple-element.5.b), custom_call_target="tpu_custom_call" | custom-call | tf_op jit(solution)/shard_map/flush/pallas_call | solution.py:914
